TPU v7x, 128 devices: a whole 4x4x4 slice. The times are simulated.
128 devices in a mesh: grp: 4 (over y), tile: 32 (over z, x, core).
Axes of the slice: x: 4, y: 4, z: 4, core: 2. Of those that a mesh axis runs over, the one named last changes fastest.
Arguments:
- tangents: float32 [2, 192, 256, 512], P(None, None, 'tile', 'grp'), may hold values from -60000 to 60000
- reaction_self: float32 [256, 512], P('tile', 'grp'), may hold values from -0.45 to -0.2
- reaction_cross: float32 [256, 512], P('tile', 'grp'), may hold values from -0.3 to -0.02
Outputs:
- corrections: float32 [24576, 192], P(('grp', 'tile'))
- growth: float32 [192], replicated
All inputs are finite; a program needn't handle non-finite values.
Results may differ from a plain program's by a relative error of at most 0.0003.
Values sent between devices are 32-bit elements; how exact they have to be, the bound alone decides.
A program may use at most 64 MiB of HBM per device.

v0:
```python
import functools
import math

import jax
import jax.numpy as jnp
from jax import lax
from jax.experimental import pallas as pl
from jax.experimental.pallas import tpu as pltpu
from jax.sharding import PartitionSpec as P

MESH = pl.DeviceIdType.MESH
F32 = jnp.float32
STEPS = 4
K = 192
NYD = 8
LANES = 128
ROWS = K + 8
BLOCKS_K = ROWS // 8
CHUNKS = 5
CHUNK = ROWS // CHUNKS
PER_CHUNK = CHUNK // 8
EDGE = STEPS
EXT = NYD + 2 * EDGE
DIFFUSION = 0.2
SLOW_RATE = 0.05
VMEM_SPEC = pl.BlockSpec(memory_space=pltpu.VMEM)
NEIGHBOURS = [(dg, dt) for dg in (-1, 0, 1) for dt in (-1, 0, 1) if (dg, dt) != (0, 0)]


def lanes_of(shape=(8, LANES)):
    return lax.broadcasted_iota(jnp.int32, shape, 1)


def pack_kernel(tan_ref, self_ref, cross_ref, t_ref, left_ref, right_ref):
    lane = lanes_of()
    sub = lax.broadcasted_iota(jnp.int32, (8, LANES), 0)

    def body(fy, _):
        f = fy // NYD
        y = fy - f * NYD
        base = f * (K * NYD) + y
        own_self = jnp.broadcast_to(self_ref[pl.ds(y, 1), :], (8, LANES))
        own_cross = jnp.broadcast_to(cross_ref[pl.ds(y, 1), :], (8, LANES))
        block = jnp.where(sub == 0, own_self, own_cross)
        left = jnp.zeros((8, LANES), F32)
        right = jnp.zeros((8, LANES), F32)
        for b in range(BLOCKS_K):
            if b > 0:
                block = tan_ref[pl.ds(base + 64 * (b - 1), 8, stride=NYD), :]
            t_ref[fy, 8 * b : 8 * b + 8, :] = block
            here = (lane >= EDGE * b) & (lane < EDGE * b + EDGE)
            left = jnp.where(here, pltpu.roll(block, EDGE * b, 1) if b else block, left)
            right = jnp.where(here, pltpu.roll(block, (EDGE * b + EDGE) % LANES, 1), right)
        left_ref[fy] = left
        right_ref[fy] = right
        return 0

    lax.fori_loop(0, 2 * NYD, body, 0)


def pack(tangents, reaction_self, reaction_cross):
    return pl.pallas_call(
        pack_kernel,
        out_shape=(
            jax.ShapeDtypeStruct((2 * NYD, ROWS, LANES), F32),
            jax.ShapeDtypeStruct((2 * NYD, 8, LANES), F32),
            jax.ShapeDtypeStruct((2 * NYD, 8, LANES), F32),
        ),
        in_specs=[VMEM_SPEC] * 3,
        out_specs=[VMEM_SPEC] * 3,
        name="pack",
    )(tangents.reshape(2 * K * NYD, LANES), reaction_self, reaction_cross)


def stencil_kernel(
    groups, tiles,
    t_ref, left_ref, right_ref, e_ref,
    up_ref, down_ref, xl_ref, xr_ref, co_ref,
    row_send, row_recv, edge_send, edge_recv,
):
    g = lax.axis_index("grp")
    t = lax.axis_index("tile")
    has = {-1: t > 0, 0: None, 1: t < tiles - 1}
    hasg = {-1: g > 0, 0: None, 1: g < groups - 1}

    def exists(dg, dt):
        terms = [c for c in (hasg[dg], has[dt]) if c is not None]
        return terms[0] if len(terms) == 1 else terms[0] & terms[1]

    barrier = pltpu.get_barrier_semaphore()
    for dg, dt in NEIGHBOURS:
        @pl.when(exists(dg, dt))
        def _():
            pl.semaphore_signal(barrier, inc=1, device_id=(g + dg, t + dt), device_id_type=MESH)
    wide_g = 1 + (g > 0).astype(jnp.int32) + (g < groups - 1).astype(jnp.int32)
    wide_t = 1 + (t > 0).astype(jnp.int32) + (t < tiles - 1).astype(jnp.int32)
    pl.semaphore_wait(barrier, wide_g * wide_t - 1)

    def row_copies(direction, c):
        rows = pl.ds(pl.multiple_of(c * CHUNK, 8), CHUNK)
        if direction == 0:
            fast, slow, dst, dt = slice(0, 4), slice(8, 11), down_ref, -1
        else:
            fast, slow, dst, dt = slice(4, 8), slice(13, 16), up_ref, 1
        out = []
        for i, (src, where) in enumerate(((fast, slice(0, 4)), (slow, slice(4, 7)))):
            out.append(
                pltpu.make_async_remote_copy(
                    src_ref=t_ref.at[src, rows, :],
                    dst_ref=dst.at[where, rows, :],
                    send_sem=row_send.at[direction, c, i],
                    recv_sem=row_recv.at[direction, c, i],
                    device_id=(g, t + dt),
                    device_id_type=MESH,
                )
            )
        return out

    def edge_copies(side, dt):
        src = left_ref if side == 0 else right_ref
        dst = xr_ref if side == 0 else xl_ref
        dg = -1 if side == 0 else 1
        rows, where = {
            -1: (slice(0, 4), slice(12, 16)),
            0: (slice(0, 8), slice(4, 12)),
            1: (slice(4, 8), slice(0, 4)),
        }[dt]
        out = []
        for f in range(2):
            out.append(
                pltpu.make_async_remote_copy(
                    src_ref=src.at[slice(8 * f + rows.start, 8 * f + rows.stop)],
                    dst_ref=dst.at[slice(EXT * f + where.start, EXT * f + where.stop)],
                    send_sem=edge_send.at[side, dt + 1, f],
                    recv_sem=edge_recv.at[side, dt + 1, f],
                    device_id=(g + dg, t + dt),
                    device_id_type=MESH,
                )
            )
        return dg, out

    for direction, dt in ((0, -1), (1, 1)):
        @pl.when(has[dt])
        def _():
            for copy in row_copies(direction, 0):
                copy.start()
    for side in range(2):
        for dt in (0, -1, 1):
            dg, copies = edge_copies(side, dt)

            @pl.when(exists(dg, dt))
            def _():
                for copy in copies:
                    copy.start()
    for direction, dt in ((0, -1), (1, 1)):
        @pl.when(has[dt])
        def _():
            def start(c, _):
                for copy in row_copies(direction, c):
                    copy.start()
                return 0

            lax.fori_loop(1, CHUNKS, start, 0)

    def wait_rows(c):
        for direction, dt in ((0, 1), (1, -1)):
            @pl.when(has[dt])
            def _():
                for copy in row_copies(direction, c):
                    copy.wait_recv()

    for side in range(2):
        for dt in (0, -1, 1):
            dg, copies = edge_copies(side, dt)

            @pl.when(exists(-dg, -dt))
            def _():
                for copy in copies:
                    copy.wait_recv()

    wait_rows(0)

    lane = lanes_of()
    zero = jnp.zeros((8, LANES), jnp.int32)
    first_lane = lane == 0
    last_lane = lane == LANES - 1
    wall_left = first_lane & (zero + g == 0)
    wall_right = last_lane & (zero + g == groups - 1)
    wall_top = zero + t == 0
    wall_bottom = zero + t == tiles - 1
    near = lane < EDGE
    far = lane >= LANES - EDGE

    def main_of(f, e, b):
        rows = pl.ds(pl.multiple_of(8 * b, 8), 8)
        if e < EDGE:
            return up_ref[e if f == 0 else 4 + e - 1, rows, :]
        if e < EDGE + NYD:
            return t_ref[NYD * f + e - EDGE, rows, :]
        return down_ref[e - 12 + 4 * f, rows, :]

    def halo_of(f, e, b):
        to_low = lax.rem(LANES - EDGE * b, LANES)
        to_high = LANES - EDGE - EDGE * b
        from_right = pltpu.roll(xr_ref[EXT * f + e], to_low, 1)
        from_left = pltpu.roll(xl_ref[EXT * f + e], to_high, 1)
        return jnp.where(near, from_right, jnp.where(far, from_left, 0.0))

    for e in range(1, EXT - 1):
        for part, block in enumerate((main_of(0, e, 0), halo_of(0, e, jnp.int32(0)))):
            own = jnp.broadcast_to(block[0:1, :], (8, LANES)) + (1.0 - 4.0 * DIFFUSION)
            co_ref[part, 0, e] = own
            co_ref[part, 1, e] = jnp.broadcast_to(block[1:2, :], (8, LANES))

    def sides(value):
        main, halo = value
        lm, lh = pltpu.roll(main, 1, 1), pltpu.roll(halo, 1, 1)
        rm, rh = pltpu.roll(main, LANES - 1, 1), pltpu.roll(halo, LANES - 1, 1)
        left = jnp.where(wall_left, main, jnp.where(first_lane, lh, lm))
        right = jnp.where(wall_right, main, jnp.where(last_lane, rh, rm))
        return (
            left + right,
            jnp.where(first_lane, lm, lh) + jnp.where(last_lane, rm, rh),
        )

    def compute(b):
        fast = [[None] * EXT for _ in range(STEPS + 1)]
        slow = [[None] * EXT for _ in range(STEPS + 1)]
        for e in range(EXT):
            fast[0][e] = (main_of(0, e, b), halo_of(0, e, b))
            if 1 <= e < EXT - 1:
                slow[0][e] = (main_of(1, e, b), halo_of(1, e, b))
            for s in range(1, STEPS + 1):
                r = e - s
                if r < s or r > EXT - 1 - s:
                    continue
                old, old_slow = fast[s - 1][r], slow[s - 1][r]
                north, south = fast[s - 1][r - 1], fast[s - 1][r + 1]
                side = sides(old)
                new, new_slow = [], []
                for part in range(2 if s < STEPS else 1):
                    up, down = north[part], south[part]
                    if r == EDGE:
                        up = jnp.where(wall_top, old[part], up)
                    if r == EDGE + NYD - 1:
                        down = jnp.where(wall_bottom, old[part], down)
                    total = (up + down) + side[part]
                    new.append(
                        co_ref[part, 0, r] * old[part]
                        + DIFFUSION * total
                        + co_ref[part, 1, r] * old_slow[part]
                    )
                    new_slow.append(old_slow[part] + SLOW_RATE * (old[part] - old_slow[part]))
                fast[s][r] = tuple(new)
                slow[s][r] = tuple(new_slow)
                if s == STEPS:
                    rows = pl.ds(pl.multiple_of(8 * (b - 1), 8), 8)
                    e_ref[r - EDGE, rows, :] = new[0]
                    e_ref[NYD + r - EDGE, rows, :] = new_slow[0]

    def chunk(first, count):
        def body(i, _):
            compute(first + i)
            return 0

        lax.fori_loop(0, count, body, 0)

    chunk(1, PER_CHUNK - 1)

    def rest(c, _):
        wait_rows(c)
        chunk(c * PER_CHUNK, PER_CHUNK)
        return 0

    lax.fori_loop(1, CHUNKS, rest, 0)

    for direction, dt in ((0, -1), (1, 1)):
        @pl.when(has[dt])
        def _():
            def finish(c, _):
                for copy in row_copies(direction, c):
                    copy.wait_send()
                return 0

            lax.fori_loop(0, CHUNKS, finish, 0)
    for side in range(2):
        for dt in (0, -1, 1):
            dg, copies = edge_copies(side, dt)

            @pl.when(exists(dg, dt))
            def _():
                for copy in copies:
                    copy.wait_send()


def stencil(groups, tiles, packed, left, right):
    return pl.pallas_call(
        functools.partial(stencil_kernel, groups, tiles),
        out_shape=jax.ShapeDtypeStruct((2 * NYD, K, LANES), F32),
        in_specs=[VMEM_SPEC] * 3,
        out_specs=VMEM_SPEC,
        scratch_shapes=[
            pltpu.VMEM((7, ROWS, LANES), F32),
            pltpu.VMEM((7, ROWS, LANES), F32),
            pltpu.VMEM((2 * EXT, 8, LANES), F32),
            pltpu.VMEM((2 * EXT, 8, LANES), F32),
            pltpu.VMEM((2, 2, EXT, 8, LANES), F32),
            pltpu.SemaphoreType.DMA((2, CHUNKS, 2)),
            pltpu.SemaphoreType.DMA((2, CHUNKS, 2)),
            pltpu.SemaphoreType.DMA((2, 3, 2)),
            pltpu.SemaphoreType.DMA((2, 3, 2)),
        ],
        compiler_params=pltpu.CompilerParams(collective_id=0, has_side_effects=True),
        name="stencil",
    )(packed, left, right)


def gram_kernel(e_ref, g_ref, p_ref):
    total = jnp.zeros((K, K), F32)
    for i in range(2 * NYD):
        a = e_ref[i]
        total = total + lax.dot_general(
            a, a, (((1,), (1,)), ((), ())),
            precision=lax.Precision.HIGHEST, preferred_element_type=F32,
        )
    g_ref[...] = total
    zeros = jnp.zeros((64, 64), F32)
    p_ref[0:64, :] = total[0:64, 0:128]
    p_ref[64:128, :] = jnp.concatenate([total[0:64, 128:192], total[64:128, 64:128]], axis=1)
    p_ref[128:192, :] = jnp.concatenate([total[64:128, 128:192], total[128:192, 128:192]], axis=1)


def gram(evolved):
    return pl.pallas_call(
        gram_kernel,
        out_shape=(jax.ShapeDtypeStruct((K, K), F32), jax.ShapeDtypeStruct((K, LANES), F32)),
        in_specs=[VMEM_SPEC],
        out_specs=[VMEM_SPEC] * 2,
        name="gram",
    )(evolved)


def reduce_kernel(groups, tiles, p_ref, o_ref, near_ref, y_ref, z_ref, sends, recvs):
    g = lax.axis_index("grp")
    t = lax.axis_index("tile")
    inner = 8
    outer = tiles // inner
    piece = K // inner
    z = t // inner
    q = t - z * inner

    def in_line(d):
        return (g, z * inner + lax.rem(q + d, inner))

    def in_y(d):
        return (lax.rem(g + d, groups), t)

    def in_z(d):
        return (g, lax.rem(z + d, outer) * inner + q)

    peers = (
        [in_line(d) for d in range(1, inner)]
        + [in_y(d) for d in range(1, groups)]
        + [in_z(d) for d in range(1, outer)]
    )
    barrier = pltpu.get_barrier_semaphore()
    for peer in peers:
        pl.semaphore_signal(barrier, inc=1, device_id=peer, device_id_type=MESH)
    pl.semaphore_wait(barrier, len(peers))

    count = [0]

    def copy_to(src, dst, peer):
        i = count[0]
        count[0] += 1
        copy = pltpu.make_async_remote_copy(
            src_ref=src, dst_ref=dst, send_sem=sends.at[i], recv_sem=recvs.at[i],
            device_id=peer, device_id_type=MESH,
        )
        copy.start()
        return copy

    def rows(index):
        return pl.ds(pl.multiple_of(index * piece, 8), piece)

    started = []
    phase = []
    for d in range(1, inner):
        phase.append(copy_to(p_ref.at[rows(lax.rem(q + d, inner))], near_ref.at[d - 1], in_line(d)))
    total = p_ref[rows(q), :]
    for d, copy in enumerate(phase):
        copy.wait_recv()
        total = total + near_ref[d]
    started += phase
    for buf, me, size, peer_of in ((y_ref, g, groups, in_y), (z_ref, z, outer, in_z)):
        buf[me] = total
        phase = [copy_to(buf.at[me], buf.at[me], peer_of(d)) for d in range(1, size)]
        for copy in phase:
            copy.wait_recv()
        total = buf[0]
        for i in range(1, size):
            total = total + buf[i]
        started += phase
    o_ref[rows(q), :] = total
    phase = [copy_to(o_ref.at[rows(q)], o_ref.at[rows(q)], in_line(d)) for d in range(1, inner)]
    for copy in phase:
        copy.wait_recv()
    started += phase
    for copy in started:
        copy.wait_send()


def reduce_all(groups, tiles, packed):
    copies = 2 * 7 + (groups - 1) + (tiles // 8 - 1)
    return pl.pallas_call(
        functools.partial(reduce_kernel, groups, tiles),
        out_shape=jax.ShapeDtypeStruct((K, LANES), F32),
        in_specs=[VMEM_SPEC],
        out_specs=VMEM_SPEC,
        scratch_shapes=[
            pltpu.VMEM((7, K // 8, LANES), F32),
            pltpu.VMEM((groups, K // 8, LANES), F32),
            pltpu.VMEM((tiles // 8, K // 8, LANES), F32),
            pltpu.SemaphoreType.DMA((copies,)),
            pltpu.SemaphoreType.DMA((copies,)),
        ],
        compiler_params=pltpu.CompilerParams(collective_id=1, has_side_effects=True),
        name="reduce",
    )(packed)


def unpack(p):
    upper = jnp.zeros((K, K), F32)
    upper = upper.at[0:64, 0:128].set(p[0:64])
    upper = upper.at[0:64, 128:192].set(p[64:128, 0:64])
    upper = upper.at[64:128, 64:128].set(p[64:128, 64:128])
    upper = upper.at[64:128, 128:192].set(p[128:192, 0:64])
    upper = upper.at[128:192, 128:192].set(p[128:192, 64:128])
    upper = jnp.triu(upper)
    return upper + jnp.triu(upper, 1).T


def per_device(groups, tiles, tangents, reaction_self, reaction_cross):
    packed, left, right = pack(tangents, reaction_self, reaction_cross)
    evolved = stencil(groups, tiles, packed, left, right)
    local_gram, local_packed = gram(evolved)
    local_factor = jnp.linalg.cholesky(local_gram)
    total = unpack(reduce_all(groups, tiles, local_packed))
    factor = jnp.linalg.cholesky(total)
    solved = jax.scipy.linalg.solve_triangular(factor, local_factor, lower=True)
    corrections = math.sqrt(groups * tiles) * solved.T
    growth = jnp.log(jnp.diagonal(factor))
    return (corrections, growth)


def solution(mesh):
    groups, tiles = mesh.shape["grp"], mesh.shape["tile"]
    in_specs = (P(None, None, "tile", "grp"), P("tile", "grp"), P("tile", "grp"))
    out_specs = (P(("grp", "tile"), None), P())
    return jax.shard_map(
        functools.partial(per_device, groups, tiles),
        mesh=mesh, in_specs=in_specs, out_specs=out_specs, check_vma=False,
    )
```

profile of v0, /device:TPU:1, one launch (start us, length us, event | category | flops | bytes accessed | tf_op | source)
XLA Modules:
  0.0 152.6 jit_solution(10610143991964898326)
XLA Ops:
  0.6 4.5 %pack.1 = (f32[16,200,128]{2,1,0:T(8,128)}, f32[16,8,128]{2,1,0:T(8,128)}, f32[16,8,128]{2,1,0:T(8,128)}) custom-call(f32[3072,128]{1,0:T(8,128)} %bitcast.47, f32[8,128]{1,0:T(8,128)} %self_ref.1, f32[8,128]{1,0:T(8,128)} %cross_ref.1), custom_call_target="tpu_custom_call" | custom-call | tf_op jit(solution)/shard_map/pack/pallas_call | solution.py:62
  5.1 23.4 %stencil.1.e_ref = f32[16,192,128]{2,1,0:T(8,128)} custom-call(f32[16,200,128]{2,1,0:T(8,128)} %get-tuple-element.68.t_ref, f32[16,8,128]{2,1,0:T(8,128)} %get-tuple-element.69.left_ref, f32[16,8,128]{2,1,0:T(8,128)} %get-tuple-element.70.right_ref), custom_call_target="tpu_custom_call" | custom-call | tf_op jit(solution)/shard_map/stencil/pallas_call | solution.py:297
  28.5 4.7 %gram.1 = (f32[192,192]{1,0:T(8,128)}, f32[192,128]{1,0:T(8,128)}) custom-call(f32[16,192,128]{2,1,0:T(8,128)} %stencil.1.e_ref), custom_call_target="tpu_custom_call" | custom-call | tf_op jit(solution)/shard_map/gram/pallas_call | solution.py:334
  33.3 23.4 %reduce.25 = f32[192,128]{1,0:T(8,128)} custom-call(f32[192,128]{1,0:T(8,128)} %get-tuple-element.71.p_ref), custom_call_target="tpu_custom_call" | custom-call | tf_op jit(solution)/shard_map/reduce/pallas_call | solution.py:415
  56.7 0.9 fusion.17
  57.6 0.1 copy.27
  57.7 0.8 slice.167
  58.4 0.1 copy.26
  58.6 0.6 fusion.18
  59.1 0.6 and_reduce_fusion
  59.8 2.0 %fusion.12 = f32[64,64]{0,1:T(8,128)S(1)} fusion(f32[64,64]{0,1:T(8,128)S(1)} %copy.27, s32[]{:T(128)} %bitcast.1, s32[]{:T(128)} %bitcast.2, f32[64,128]{0,1:T(8,128)S(1)} %copy.26, pred[]{:T(512)} %and_reduce_fusion), kind=kLoop, calls=%fused_computation.37 | loop fusion | flops 4096 | bytes 65545 | tf_op jit(solution)/shard_map/select.18
  61.8 2.1 %scatter.19 = f32[192,192]{0,1:T(8,128)S(1)} dynamic-update-slice(f32[192,192]{0,1:T(8,128)S(1)} %scatter.16, f32[64,64]{0,1:T(8,128)S(1)} %fusion.12, s32[]{:T(128)} %bitcast.1, s32[]{:T(128)} %bitcast.2) | dynamic-update-slice | bytes 32772 | tf_op jit(solution)/shard_map/scatter | solution.py:435
  63.9 0.1 copy.28
  64.0 1.4 scatter.20
  65.4 0.1 copy.29
  65.5 1.1 scatter.21
  66.6 0.1 copy.30
  66.7 0.1 copy.21
  66.9 0.0 copy-start
  66.9 0.1 copy.22
  67.1 11.7 %cholesky.136 = f32[128,128]{1,0:T(8,128)S(1)} custom-call(f32[128,128]{1,0:T(8,128)S(1)} %cholesky.208), custom_call_target="Cholesky" | custom-call | tf_op jit(solution)/shard_map/jit(cholesky)/cholesky | solution.py:449
  78.8 9.8 %custom-call.16 = f32[1,128,128]{1,2,0:T(8,128)S(1)} custom-call(f32[1,128,128]{2,1,0:T(8,128)S(1)} %get-tuple-element.100), custom_call_target="InvertDiagBlocksLowerTriangular" | custom-call | tf_op jit(solution)/shard_map/jit(cholesky)/cholesky | solution.py:449
  88.7 0.2 constant_dynamic-update-slice_fusion.3
  88.8 0.2 convolution_subtract_fusion.2
  89.0 5.8 %cholesky.156 = f32[64,64]{1,0:T(8,128)S(1)} custom-call(f32[64,64]{1,0:T(8,128)S(1)} %convolution_subtract_fusion.2), custom_call_target="Cholesky" | custom-call | tf_op jit(solution)/shard_map/jit(cholesky)/cholesky | solution.py:449
  94.9 0.7 compare_reduce_fusion.2
  95.6 0.6 compare_reduce_fusion.3
  97.7 0.1 fusion.7
  97.8 19.9 %custom-call.12 = f32[2,128,128]{1,2,0:T(8,128)S(1)} custom-call(f32[2,128,128]{2,1,0:T(8,128)S(1)} %pad_maximum_fusion), custom_call_target="InvertDiagBlocksLowerTriangular" | custom-call | tf_op jit(solution)/shard_map/jit(_solve_triangular)/triangular_solve | solution.py:450
  117.7 0.0 copy-done
  117.7 0.1 copy.23
  117.9 11.7 %cholesky.174 = f32[128,128]{1,0:T(8,128)S(1)} custom-call(f32[128,128]{1,0:T(8,128)S(1)} %cholesky.211), custom_call_target="Cholesky" | custom-call | tf_op jit(solution)/shard_map/jit(cholesky)/cholesky | solution.py:447
  129.6 9.8 %custom-call.17 = f32[1,128,128]{1,2,0:T(8,128)S(1)} custom-call(f32[1,128,128]{2,1,0:T(8,128)S(1)} %get-tuple-element.102), custom_call_target="InvertDiagBlocksLowerTriangular" | custom-call | tf_op jit(solution)/shard_map/jit(cholesky)/cholesky | solution.py:447
  139.5 0.2 constant_dynamic-update-slice_fusion.1
  139.7 0.2 convolution_subtract_fusion.1
  139.9 5.8 %cholesky.194 = f32[64,64]{1,0:T(8,128)S(1)} custom-call(f32[64,64]{1,0:T(8,128)S(1)} %convolution_subtract_fusion.1), custom_call_target="Cholesky" | custom-call | tf_op jit(solution)/shard_map/jit(cholesky)/cholesky | solution.py:447
  145.7 0.6 compare_reduce_fusion
  146.4 0.6 compare_reduce_fusion.1
  148.3 0.4 fusion.5
  148.7 0.3 convolution_subtract_fusion
  149.1 0.3 fusion.14
  149.4 0.7 fusion
  150.1 1.9 %gather_fusion = f32[192]{0:T(256)S(1)} fusion(f32[192,192]{1,0:T(8,128)S(1)} %get-tuple-element.94, s32[192]{0:T(256)S(1)} %bitcast.46), kind=kCustom, calls=%fused_computation | custom fusion | bytes 3072 | tf_op jit(solution)/shard_map/jit(diagonal)/cond/branch_0_fun/gather | solution.py:452
  152.0 0.6 log.3
  (23 shorter events, 0.4 us)
Async XLA Ops:
  66.9 50.8 %copy-start = (f32[192,192]{1,0:T(8,128)S(1)}, f32[192,192]{1,0:T(8,128)}, u32[]{:S(2)}) copy-start(f32[192,192]{1,0:T(8,128)} %get-tuple-element.72) | copy-start | bytes 442372
where the time goes:
time: 153 us
  other arithmetic  81 us (53%)
  Pallas kernels  56 us (37%)
  local copies, waits for them, and re-layouts  10.2 us (7%)
  between operations  3.59 us (2%)
  matrix products  1.77 us (1%)
    another operation x7, other arithmetic, per_device(): factor = jnp.linalg.cholesky(total)  28.8 us
    another operation x7, other arithmetic, per_device(): local_factor = jnp.linalg.cholesky(local_gram)  28.7 us
    pallas_call x1, Pallas kernels, reduce_all(): pl.pallas_call(functools.partial(reduce_kernel, groups, tiles), out_shape...  23.4 us
    pallas_call x1, Pallas kernels, stencil(): pl.pallas_call(functools.partial(stencil_kernel, groups, tiles), out_shap...  23.4 us
    another operation x6, other arithmetic, per_device(): solved = jax.scipy.linalg.solve_triangular(factor, local_factor, lower=True)  20 us
    pallas_call x1, Pallas kernels, gram(): pl.pallas_call(gram_kernel, out_shape=(jax.ShapeDtypeStruct((K, K), F32),...  4.72 us
    pallas_call x1, Pallas kernels, pack(): pl.pallas_call(pack_kernel, out_shape=(jax.ShapeDtypeStruct((2 * NYD, ROW...  4.5 us

commit v1 on v0

--- a/solution.py
+++ b/solution.py
@@ -317,8 +317,8 @@
 
 def gram_kernel(e_ref, g_ref, p_ref):
     total = jnp.zeros((K, K), F32)
-    for i in range(2 * NYD):
-        a = e_ref[i]
+    for i in range(NYD):
+        a = jnp.concatenate([e_ref[i], e_ref[NYD + i]], axis=1)
         total = total + lax.dot_general(
             a, a, (((1,), (1,)), ((), ())),
             precision=lax.Precision.HIGHEST, preferred_element_type=F32,
@@ -429,28 +429,146 @@
     )(packed)
 
 
-def unpack(p):
-    upper = jnp.zeros((K, K), F32)
-    upper = upper.at[0:64, 0:128].set(p[0:64])
-    upper = upper.at[0:64, 128:192].set(p[64:128, 0:64])
-    upper = upper.at[64:128, 64:128].set(p[64:128, 64:128])
-    upper = upper.at[64:128, 128:192].set(p[128:192, 0:64])
-    upper = upper.at[128:192, 128:192].set(p[128:192, 64:128])
-    upper = jnp.triu(upper)
-    return upper + jnp.triu(upper, 1).T
+def eliminate(w_ref, emit, invert):
+    lane = lanes_of()
+    sub = lax.broadcasted_iota(jnp.int32, (8, LANES), 0)
+    panels = K // 8
+    for p in range(panels):
+        j0 = 8 * p
+        h, l0 = j0 // LANES, j0 % LANES
+        halves = (0, 1) if invert else tuple(range(h, 2))
+        inside = (lane >= l0) & (lane < l0 + 8)
+        blk = {v: w_ref[j0 : j0 + 8, LANES * v : LANES * v + LANES] for v in halves}
+        cols = [jnp.broadcast_to(blk[h][:, l0 + i : l0 + i + 1], (8, LANES)) for i in range(8)]
+        el = [
+            [jnp.broadcast_to(cols[i][m : m + 1, :], (8, LANES)) if m >= i else None for i in range(8)]
+            for m in range(8)
+        ]
+        if invert:
+            blk[h] = jnp.where(inside, jnp.where(lane - l0 == sub, 1.0, 0.0), blk[h])
+        rows = {v: [jnp.broadcast_to(blk[v][m : m + 1, :], (8, LANES)) for m in range(8)] for v in halves}
+        fac = [[None] * 8 for _ in range(8)]
+        r, r2, pivots = [], [], []
+        for i in range(8):
+            pivots.append(el[i][i])
+            r.append(lax.rsqrt(el[i][i]))
+            r2.append(r[i] * r[i])
+            for m in range(i + 1, 8):
+                fac[m][i] = el[m][i] * r2[i]
+            for k in range(i + 1, 8):
+                for m in range(k, 8):
+                    el[m][k] = el[m][k] - fac[k][i] * el[m][i]
+            for v in halves:
+                for m in range(i + 1, 8):
+                    rows[v][m] = rows[v][m] - fac[m][i] * rows[v][i]
+        for v in halves:
+            out = rows[v][0] * r[0]
+            for i in range(1, 8):
+                out = jnp.where(sub == i, rows[v][i] * r[i], out)
+            emit(p, v, out, lane, sub)
+        emit(p, None, pivots, lane, sub)
+        if p == panels - 1:
+            break
+        z = {v: [None] * 8 for v in halves}
+        for v in halves:
+            for i in range(7, -1, -1):
+                acc = rows[v][i] * r2[i]
+                for m in range(7, i, -1):
+                    acc = acc - fac[m][i] * z[v][m]
+                z[v][i] = acc
+        for s in range(p + 1, panels):
+            rng = slice(8 * s, 8 * s + 8)
+            src = w_ref[rng, LANES * h : LANES * h + LANES]
+            low = [jnp.broadcast_to(src[:, l0 + i : l0 + i + 1], (8, LANES)) for i in range(8)]
+            for v in halves:
+                if v == h:
+                    cur = jnp.where(inside, 0.0, src) if invert else src
+                else:
+                    cur = w_ref[rng, LANES * v : LANES * v + LANES]
+                a = low[0] * z[v][0]
+                b = low[1] * z[v][1]
+                for i in range(2, 8, 2):
+                    a = a + low[i] * z[v][i]
+                    b = b + low[i + 1] * z[v][i + 1]
+                w_ref[rng, LANES * v : LANES * v + LANES] = cur - (a + b)
+
+
+def factor_kernel(a_ref, r_ref, w_ref):
+    w_ref[...] = jnp.zeros_like(w_ref)
+    w_ref[:, 0:K] = a_ref[...]
+    r_ref[...] = jnp.zeros_like(r_ref)
+
+    def emit(p, v, out, lane, sub):
+        if v is None:
+            return
+        value = jnp.where(lane + LANES * v >= sub + 8 * p, out, 0.0)
+        if v == 0:
+            r_ref[8 * p : 8 * p + 8, 0:LANES] = value
+        else:
+            r_ref[8 * p : 8 * p + 8, LANES:K] = value[:, 0 : K - LANES]
+
+    eliminate(w_ref, emit, False)
+
+
+def factor(local_gram):
+    return pl.pallas_call(
+        factor_kernel,
+        out_shape=jax.ShapeDtypeStruct((K, K), F32),
+        in_specs=[VMEM_SPEC],
+        out_specs=VMEM_SPEC,
+        scratch_shapes=[pltpu.VMEM((K, 2 * LANES), F32)],
+        name="factor",
+    )(local_gram)
+
+
+def solve_kernel(scale, p_ref, r_ref, c_ref, growth_ref, w_ref, inv_ref):
+    u0, u1, u2 = p_ref[0:64, :], p_ref[64:128, :], p_ref[128:192, :]
+    t0, t1, t2 = jnp.transpose(u0), jnp.transpose(u1), jnp.transpose(u2)
+    w_ref[0:64, 0:LANES] = u0
+    w_ref[0:64, LANES:] = u1
+    w_ref[64:128, 0:LANES] = jnp.concatenate([t0[64:128], u1[:, 64:128]], axis=1)
+    w_ref[64:128, LANES:] = u2
+    w_ref[128:192, 0:LANES] = jnp.concatenate([t1[0:64], t2[0:64]], axis=1)
+    w_ref[128:192, LANES:] = pltpu.roll(u2, 64, 1)
+    diagonal = [jnp.ones((8, LANES), F32), jnp.ones((8, LANES), F32)]
+
+    def emit(p, v, out, lane, sub):
+        if v is None:
+            h, l0 = 8 * p // LANES, 8 * p % LANES
+            for i in range(8):
+                diagonal[h] = jnp.where(lane == l0 + i, out[i], diagonal[h])
+            return
+        value = jnp.where(lane + LANES * v <= sub + 8 * p, out, 0.0)
+        inv_ref[8 * p : 8 * p + 8, LANES * v : LANES * v + LANES] = value
+
+    eliminate(w_ref, emit, True)
+    growth_ref[0:1, 0:LANES] = 0.5 * jnp.log(diagonal[0][0:1, :])
+    growth_ref[0:1, LANES:K] = 0.5 * jnp.log(diagonal[1][0:1, 0 : K - LANES])
+    c_ref[...] = scale * lax.dot_general(
+        r_ref[...], inv_ref[:, 0:K], (((1,), (1,)), ((), ())),
+        precision=lax.Precision.HIGHEST, preferred_element_type=F32,
+    )
+
+
+def solve(scale, packed, local_factor):
+    return pl.pallas_call(
+        functools.partial(solve_kernel, scale),
+        out_shape=(jax.ShapeDtypeStruct((K, K), F32), jax.ShapeDtypeStruct((1, K), F32)),
+        in_specs=[VMEM_SPEC] * 2,
+        out_specs=[VMEM_SPEC] * 2,
+        scratch_shapes=[pltpu.VMEM((K, 2 * LANES), F32)] * 2,
+        name="solve",
+    )(packed, local_factor)
 
 
 def per_device(groups, tiles, tangents, reaction_self, reaction_cross):
     packed, left, right = pack(tangents, reaction_self, reaction_cross)
     evolved = stencil(groups, tiles, packed, left, right)
     local_gram, local_packed = gram(evolved)
-    local_factor = jnp.linalg.cholesky(local_gram)
-    total = unpack(reduce_all(groups, tiles, local_packed))
-    factor = jnp.linalg.cholesky(total)
-    solved = jax.scipy.linalg.solve_triangular(factor, local_factor, lower=True)
-    corrections = math.sqrt(groups * tiles) * solved.T
-    growth = jnp.log(jnp.diagonal(factor))
-    return (corrections, growth)
+    local_factor = factor(local_gram)
+    total = reduce_all(groups, tiles, local_packed)
+    corrections, growth = solve(math.sqrt(groups * tiles), total, local_factor)
+    return (corrections, growth.reshape(K))
 
 
 def solution(mesh):

time: 153 us -> 74.4 us (0.49)
  other arithmetic: 81 us -> 0 us
  Pallas kernels: 56 us -> 73.5 us
  local copies, waits for them, and re-layouts: 10.2 us -> 0 us
  between operations: 3.59 us -> 0.65 us
  matrix products: 1.77 us -> 0 us
    another operation x23 -> x0, other arithmetic: 80.2 us -> none  [the longest x7 28.8 us: per_device(): factor = jnp.linalg.cholesky(total)]
    pallas_call x0 -> x2, Pallas kernels: none -> 18.6 us  [the longest x1 9.68 us: solve(): pl.pallas_call(functools.partial(solve_kernel, scale), out_shape=(jax.Sha...]
    scatter x5 -> x0, local copies, waits for them, and re-layouts: 4.66 us -> none  [the longest x1 2.14 us: unpack(): upper = upper.at[0:64, 128:192].set(p[64:128, 0:64])]
    gather x1 -> x0, local copies, waits for them, and re-layouts: 1.91 us -> none  [per_device(): growth = jnp.log(jnp.diagonal(factor))]
    another operation x7 -> x0, matrix products: 1.77 us -> none  [the longest x3 1.04 us: per_device(): solved = jax.scipy.linalg.solve_triangular(factor, local_factor, lower=True)]
    slice x2 -> x0, local copies, waits for them, and re-layouts: 1.69 us -> none  [the longest x1 0.92 us: unpack(): upper = upper.at[128:192, 128:192].set(p[128:192, 64:128])]
where the time goes in v1:
time: 74.4 us; the launch traced here: 74.2 us
  Pallas kernels  73.5 us (99%)
    pallas_call x1, Pallas kernels, reduce_all(): pl.pallas_call(functools.partial(reduce_kernel, groups, tiles), out_shape...  23.4 us
    pallas_call x1, Pallas kernels, stencil(): pl.pallas_call(functools.partial(stencil_kernel, groups, tiles), out_shap...  23.4 us
    pallas_call x1, Pallas kernels, solve(): pl.pallas_call(functools.partial(solve_kernel, scale), out_shape=(jax.Sha...  9.68 us
    pallas_call x1, Pallas kernels, factor(): pl.pallas_call(factor_kernel, out_shape=jax.ShapeDtypeStruct((K, K), F32)...  8.96 us
    pallas_call x1, Pallas kernels, pack(): pl.pallas_call(pack_kernel, out_shape=(jax.ShapeDtypeStruct((2 * NYD, ROW...  4.5 us
    pallas_call x1, Pallas kernels, gram(): pl.pallas_call(gram_kernel, out_shape=(jax.ShapeDtypeStruct((K, K), F32),...  3.57 us

profile of v1, /device:TPU:1, one launch (start us, length us, event | category | flops | bytes accessed | tf_op | source)
XLA Modules:
  0.0 74.2 jit_solution(4504234612628370992)
XLA Ops:
  0.6 4.5 %pack.1 = (f32[16,200,128]{2,1,0:T(8,128)}, f32[16,8,128]{2,1,0:T(8,128)}, f32[16,8,128]{2,1,0:T(8,128)}) custom-call(f32[3072,128]{1,0:T(8,128)} %bitcast.2, f32[8,128]{1,0:T(8,128)} %self_ref.1, f32[8,128]{1,0:T(8,128)} %cross_ref.1), custom_call_target="tpu_custom_call" | custom-call | tf_op jit(solution)/shard_map/pack/pallas_call | solution.py:62
  5.1 23.4 %stencil.1.e_ref = f32[16,192,128]{2,1,0:T(8,128)} custom-call(f32[16,200,128]{2,1,0:T(8,128)} %get-tuple-element.9.t_ref, f32[16,8,128]{2,1,0:T(8,128)} %get-tuple-element.10.left_ref, f32[16,8,128]{2,1,0:T(8,128)} %get-tuple-element.11.right_ref), custom_call_target="tpu_custom_call" | custom-call | tf_op jit(solution)/shard_map/stencil/pallas_call | solution.py:297
  28.5 3.6 %gram.1 = (f32[192,192]{1,0:T(8,128)}, f32[192,128]{1,0:T(8,128)}) custom-call(f32[16,192,128]{2,1,0:T(8,128)} %stencil.1.e_ref), custom_call_target="tpu_custom_call" | custom-call | tf_op jit(solution)/shard_map/gram/pallas_call | solution.py:334
  32.1 23.4 %reduce.1.p_ref = f32[192,128]{1,0:T(8,128)} custom-call(f32[192,128]{1,0:T(8,128)} %get-tuple-element.12.p_ref), custom_call_target="tpu_custom_call" | custom-call | tf_op jit(solution)/shard_map/reduce/pallas_call | solution.py:415
  55.5 9.0 %factor.1.r_ref = f32[192,192]{1,0:T(8,128)} custom-call(f32[192,192]{1,0:T(8,128)} %get-tuple-element.13.a_ref), custom_call_target="tpu_custom_call" | custom-call | tf_op jit(solution)/shard_map/factor/pallas_call | solution.py:514
  64.5 9.7 %solve.1 = (f32[192,192]{1,0:T(8,128)}, f32[1,192]{1,0:T(1,128)}) custom-call(f32[192,128]{1,0:T(8,128)} %reduce.1.p_ref, f32[192,192]{1,0:T(8,128)} %factor.1.r_ref), custom_call_target="tpu_custom_call" | custom-call | tf_op jit(solution)/shard_map/solve/pallas_call | solution.py:554

commit v2 on v0

--- a/solution.py
+++ b/solution.py
@@ -23,6 +23,7 @@
 EXT = NYD + 2 * EDGE
 DIFFUSION = 0.2
 SLOW_RATE = 0.05
+LIMIT = 12 << 20
 VMEM_SPEC = pl.BlockSpec(memory_space=pltpu.VMEM)
 NEIGHBOURS = [(dg, dt) for dg in (-1, 0, 1) for dt in (-1, 0, 1) if (dg, dt) != (0, 0)]
 
@@ -68,6 +69,7 @@
         ),
         in_specs=[VMEM_SPEC] * 3,
         out_specs=[VMEM_SPEC] * 3,
+        compiler_params=pltpu.CompilerParams(vmem_limit_bytes=LIMIT),
         name="pack",
     )(tangents.reshape(2 * K * NYD, LANES), reaction_self, reaction_cross)
 
@@ -310,37 +312,102 @@
             pltpu.SemaphoreType.DMA((2, 3, 2)),
             pltpu.SemaphoreType.DMA((2, 3, 2)),
         ],
-        compiler_params=pltpu.CompilerParams(collective_id=0, has_side_effects=True),
+        compiler_params=pltpu.CompilerParams(collective_id=0, has_side_effects=True, vmem_limit_bytes=LIMIT),
         name="stencil",
     )(packed, left, right)
 
 
-def gram_kernel(e_ref, g_ref, p_ref):
-    total = jnp.zeros((K, K), F32)
-    for i in range(2 * NYD):
-        a = e_ref[i]
-        total = total + lax.dot_general(
-            a, a, (((1,), (1,)), ((), ())),
-            precision=lax.Precision.HIGHEST, preferred_element_type=F32,
-        )
-    g_ref[...] = total
-    zeros = jnp.zeros((64, 64), F32)
-    p_ref[0:64, :] = total[0:64, 0:128]
-    p_ref[64:128, :] = jnp.concatenate([total[0:64, 128:192], total[64:128, 64:128]], axis=1)
-    p_ref[128:192, :] = jnp.concatenate([total[64:128, 128:192], total[128:192, 128:192]], axis=1)
-
-
-def gram(evolved):
-    return pl.pallas_call(
-        gram_kernel,
-        out_shape=(jax.ShapeDtypeStruct((K, K), F32), jax.ShapeDtypeStruct((K, LANES), F32)),
-        in_specs=[VMEM_SPEC],
-        out_specs=[VMEM_SPEC] * 2,
-        name="gram",
-    )(evolved)
-
-
-def reduce_kernel(groups, tiles, p_ref, o_ref, near_ref, y_ref, z_ref, sends, recvs):
+def eliminate(w_ref, emit, invert):
+    lane = lanes_of()
+    sub = lax.broadcasted_iota(jnp.int32, (8, LANES), 0)
+    panels = K // 8
+    for p in range(panels):
+        j0 = 8 * p
+        h, l0 = j0 // LANES, j0 % LANES
+        halves = (0, 1) if invert else tuple(range(h, 2))
+        inside = (lane >= l0) & (lane < l0 + 8)
+        blk = {v: w_ref[j0 : j0 + 8, LANES * v : LANES * v + LANES] for v in halves}
+        cols = [jnp.broadcast_to(blk[h][:, l0 + i : l0 + i + 1], (8, LANES)) for i in range(8)]
+        el = [
+            [jnp.broadcast_to(cols[i][m : m + 1, :], (8, LANES)) if m >= i else None for i in range(8)]
+            for m in range(8)
+        ]
+        if invert:
+            blk[h] = jnp.where(inside, jnp.where(lane - l0 == sub, 1.0, 0.0), blk[h])
+        rows = {v: [jnp.broadcast_to(blk[v][m : m + 1, :], (8, LANES)) for m in range(8)] for v in halves}
+        fac = [[None] * 8 for _ in range(8)]
+        r, r2, pivots = [], [], []
+        for i in range(8):
+            pivots.append(el[i][i])
+            r.append(lax.rsqrt(el[i][i]))
+            r2.append(r[i] * r[i])
+            for m in range(i + 1, 8):
+                fac[m][i] = el[m][i] * r2[i]
+            for k in range(i + 1, 8):
+                for m in range(k, 8):
+                    el[m][k] = el[m][k] - fac[k][i] * el[m][i]
+            for v in halves:
+                for m in range(i + 1, 8):
+                    rows[v][m] = rows[v][m] - fac[m][i] * rows[v][i]
+        for v in halves:
+            out = rows[v][0] * r[0]
+            for i in range(1, 8):
+                out = jnp.where(sub == i, rows[v][i] * r[i], out)
+            emit(p, v, out, lane, sub)
+        emit(p, None, pivots, lane, sub)
+        if p == panels - 1:
+            break
+        z = {v: [None] * 8 for v in halves}
+        for v in halves:
+            for i in range(7, -1, -1):
+                acc = rows[v][i] * r2[i]
+                for m in range(7, i, -1):
+                    acc = acc - fac[m][i] * z[v][m]
+                z[v][i] = acc
+        for s in range(p + 1, panels):
+            rng = slice(8 * s, 8 * s + 8)
+            src = w_ref[rng, LANES * h : LANES * h + LANES]
+            low = [jnp.broadcast_to(src[:, l0 + i : l0 + i + 1], (8, LANES)) for i in range(8)]
+            for v in halves:
+                if v == h:
+                    cur = jnp.where(inside, 0.0, src) if invert else src
+                else:
+                    cur = w_ref[rng, LANES * v : LANES * v + LANES]
+                a = low[0] * z[v][0]
+                b = low[1] * z[v][1]
+                for i in range(2, 8, 2):
+                    a = a + low[i] * z[v][i]
+                    b = b + low[i + 1] * z[v][i + 1]
+                w_ref[rng, LANES * v : LANES * v + LANES] = cur - (a + b)
+        yield
+
+
+def split(a):
+    high = a.astype(jnp.bfloat16)
+    rest = a - high.astype(F32)
+    middle = rest.astype(jnp.bfloat16)
+    return high, middle, (rest - middle.astype(F32)).astype(jnp.bfloat16)
+
+
+def gram_of(e_ref):
+    def product(a, b):
+        return lax.dot_general(a, b, (((1,), (1,)), ((), ())), preferred_element_type=F32)
+
+    same = jnp.zeros((K, K), F32)
+    mixed = jnp.zeros((K, K), F32)
+    for y in range(NYD):
+        a = jnp.concatenate([e_ref[y], e_ref[NYD + y]], axis=1)
+        high, middle, low = split(a)
+        same = same + product(high, high) + product(middle, middle)
+        mixed = mixed + product(high, middle) + product(high, low)
+    return same + mixed + jnp.transpose(mixed)
+
+
+def tail_kernel(
+    groups, tiles,
+    e_ref, o_ref, r_ref,
+    p_ref, near_ref, y_ref, z_ref, w_ref, sends, recvs,
+):
     g = lax.axis_index("grp")
     t = lax.axis_index("tile")
     inner = 8
@@ -366,6 +433,14 @@
     barrier = pltpu.get_barrier_semaphore()
     for peer in peers:
         pl.semaphore_signal(barrier, inc=1, device_id=peer, device_id_type=MESH)
+
+    gram = gram_of(e_ref)
+    w_ref[:, 0:LANES] = gram[:, 0:LANES]
+    w_ref[:, LANES:K] = gram[:, LANES:K]
+    w_ref[:, K : 2 * LANES] = jnp.zeros((K, 2 * LANES - K), F32)
+    p_ref[0:64, :] = gram[0:64, 0:128]
+    p_ref[64:128, :] = jnp.concatenate([gram[0:64, 128:192], gram[64:128, 64:128]], axis=1)
+    p_ref[128:192, :] = jnp.concatenate([gram[64:128, 128:192], gram[128:192, 128:192]], axis=1)
     pl.semaphore_wait(barrier, len(peers))
 
     count = [0]
@@ -383,10 +458,24 @@
     def rows(index):
         return pl.ds(pl.multiple_of(index * piece, 8), piece)
 
+    def emit_factor(p, v, out, lane, sub):
+        if v is None:
+            return
+        value = jnp.where(lane + LANES * v >= sub + 8 * p, out, 0.0)
+        r_ref[8 * p : 8 * p + 8, LANES * v : LANES * v + LANES] = value
+
+    r_ref[...] = jnp.zeros_like(r_ref)
+    local = eliminate(w_ref, emit_factor, False)
+
+    def advance(panels):
+        for _ in range(panels):
+            next(local, None)
+
     started = []
     phase = []
     for d in range(1, inner):
         phase.append(copy_to(p_ref.at[rows(lax.rem(q + d, inner))], near_ref.at[d - 1], in_line(d)))
+    advance(6)
     total = p_ref[rows(q), :]
     for d, copy in enumerate(phase):
         copy.wait_recv()
@@ -395,6 +484,7 @@
     for buf, me, size, peer_of in ((y_ref, g, groups, in_y), (z_ref, z, outer, in_z)):
         buf[me] = total
         phase = [copy_to(buf.at[me], buf.at[me], peer_of(d)) for d in range(1, size)]
+        advance(5)
         for copy in phase:
             copy.wait_recv()
         total = buf[0]
@@ -403,6 +493,7 @@
         started += phase
     o_ref[rows(q), :] = total
     phase = [copy_to(o_ref.at[rows(q)], o_ref.at[rows(q)], in_line(d)) for d in range(1, inner)]
+    advance(K // 8)
     for copy in phase:
         copy.wait_recv()
     started += phase
@@ -410,47 +501,75 @@
         copy.wait_send()
 
 
-def reduce_all(groups, tiles, packed):
+def solve_kernel(scale, o_ref, r_ref, c_ref, growth_ref, v_ref, inv_ref):
+    u0, u1, u2 = o_ref[0:64, :], o_ref[64:128, :], o_ref[128:192, :]
+    t0, t1, t2 = jnp.transpose(u0), jnp.transpose(u1), jnp.transpose(u2)
+    v_ref[0:64, 0:LANES] = u0
+    v_ref[0:64, LANES:] = u1
+    v_ref[64:128, 0:LANES] = jnp.concatenate([t0[64:128], u1[:, 64:128]], axis=1)
+    v_ref[64:128, LANES:] = u2
+    v_ref[128:192, 0:LANES] = jnp.concatenate([t1[0:64], t2[0:64]], axis=1)
+    v_ref[128:192, LANES:] = pltpu.roll(u2, 64, 1)
+    diagonal = [jnp.ones((8, LANES), F32), jnp.ones((8, LANES), F32)]
+
+    def emit_inverse(p, v, out, lane, sub):
+        if v is None:
+            h, l0 = 8 * p // LANES, 8 * p % LANES
+            for i in range(8):
+                diagonal[h] = jnp.where(lane == l0 + i, out[i], diagonal[h])
+            return
+        value = jnp.where(lane + LANES * v <= sub + 8 * p, out, 0.0)
+        inv_ref[8 * p : 8 * p + 8, LANES * v : LANES * v + LANES] = value
+
+    for _ in eliminate(v_ref, emit_inverse, True):
+        pass
+    growth_ref[0:1, 0:LANES] = 0.5 * jnp.log(diagonal[0][0:1, :])
+    growth_ref[0:1, LANES:K] = 0.5 * jnp.log(diagonal[1][0:1, 0 : K - LANES])
+    c_ref[...] = scale * lax.dot_general(
+        r_ref[...], inv_ref[...], (((1,), (1,)), ((), ())),
+        precision=lax.Precision.HIGHEST, preferred_element_type=F32,
+    )
+
+
+def tail(groups, tiles, evolved):
     copies = 2 * 7 + (groups - 1) + (tiles // 8 - 1)
     return pl.pallas_call(
-        functools.partial(reduce_kernel, groups, tiles),
-        out_shape=jax.ShapeDtypeStruct((K, LANES), F32),
+        functools.partial(tail_kernel, groups, tiles),
+        out_shape=(jax.ShapeDtypeStruct((K, LANES), F32), jax.ShapeDtypeStruct((K, 2 * LANES), F32)),
         in_specs=[VMEM_SPEC],
-        out_specs=VMEM_SPEC,
+        out_specs=[VMEM_SPEC] * 2,
         scratch_shapes=[
+            pltpu.VMEM((K, LANES), F32),
             pltpu.VMEM((7, K // 8, LANES), F32),
             pltpu.VMEM((groups, K // 8, LANES), F32),
             pltpu.VMEM((tiles // 8, K // 8, LANES), F32),
+            pltpu.VMEM((K, 2 * LANES), F32),
             pltpu.SemaphoreType.DMA((copies,)),
             pltpu.SemaphoreType.DMA((copies,)),
         ],
-        compiler_params=pltpu.CompilerParams(collective_id=1, has_side_effects=True),
-        name="reduce",
-    )(packed)
-
-
-def unpack(p):
-    upper = jnp.zeros((K, K), F32)
-    upper = upper.at[0:64, 0:128].set(p[0:64])
-    upper = upper.at[0:64, 128:192].set(p[64:128, 0:64])
-    upper = upper.at[64:128, 64:128].set(p[64:128, 64:128])
-    upper = upper.at[64:128, 128:192].set(p[128:192, 0:64])
-    upper = upper.at[128:192, 128:192].set(p[128:192, 64:128])
-    upper = jnp.triu(upper)
-    return upper + jnp.triu(upper, 1).T
+        compiler_params=pltpu.CompilerParams(collective_id=1, has_side_effects=True, vmem_limit_bytes=LIMIT),
+        name="tail",
+    )(evolved)
+
+
+def solve(scale, reduced, local_factor):
+    return pl.pallas_call(
+        functools.partial(solve_kernel, scale),
+        out_shape=(jax.ShapeDtypeStruct((K, K), F32), jax.ShapeDtypeStruct((1, K), F32)),
+        in_specs=[VMEM_SPEC] * 2,
+        out_specs=[VMEM_SPEC] * 2,
+        scratch_shapes=[pltpu.VMEM((K, 2 * LANES), F32)] * 2,
+        compiler_params=pltpu.CompilerParams(vmem_limit_bytes=LIMIT),
+        name="solve",
+    )(reduced, local_factor)
 
 
 def per_device(groups, tiles, tangents, reaction_self, reaction_cross):
     packed, left, right = pack(tangents, reaction_self, reaction_cross)
     evolved = stencil(groups, tiles, packed, left, right)
-    local_gram, local_packed = gram(evolved)
-    local_factor = jnp.linalg.cholesky(local_gram)
-    total = unpack(reduce_all(groups, tiles, local_packed))
-    factor = jnp.linalg.cholesky(total)
-    solved = jax.scipy.linalg.solve_triangular(factor, local_factor, lower=True)
-    corrections = math.sqrt(groups * tiles) * solved.T
-    growth = jnp.log(jnp.diagonal(factor))
-    return (corrections, growth)
+    reduced, local_factor = tail(groups, tiles, evolved)
+    corrections, growth = solve(math.sqrt(groups * tiles), reduced, local_factor)
+    return (corrections, growth.reshape(K))
 
 
 def solution(mesh):

time: 153 us -> 57.3 us (0.37)
  other arithmetic: 81 us -> 0 us
  local copies, waits for them, and re-layouts: 10.2 us -> 2.77 us
  between operations: 3.59 us -> 0.66 us
  Pallas kernels: 56 us -> 53.6 us
  matrix products: 1.77 us -> 0 us
    another operation x23 -> x0, other arithmetic: 80.2 us -> none  [the longest x7 28.8 us: per_device(): factor = jnp.linalg.cholesky(total)]
    scatter x5 -> x0, local copies, waits for them, and re-layouts: 4.66 us -> none  [the longest x1 2.14 us: unpack(): upper = upper.at[0:64, 128:192].set(p[64:128, 0:64])]
    pallas_call x2, Pallas kernels: 28.1 us -> 30.8 us  [the longest x1 22.1 us: tail(): pl.pallas_call(functools.partial(tail_kernel, groups, tiles), out_shape=(...]
    pallas_call x1, Pallas kernels: 4.5 us -> 1.97 us  [pack(): pl.pallas_call(pack_kernel, out_shape=(jax.ShapeDtypeStruct((2 * NYD, ROW...]
    pallas_call x1, Pallas kernels: 23.4 us -> 20.9 us  [stencil(): pl.pallas_call(functools.partial(stencil_kernel, groups, tiles), out_shap...]
    unnamed x7 -> x6, local copies, waits for them, and re-layouts: 0.4 us -> 2.77 us
    gather x1 -> x0, local copies, waits for them, and re-layouts: 1.91 us -> none  [per_device(): growth = jnp.log(jnp.diagonal(factor))]
    another operation x7 -> x0, matrix products: 1.77 us -> none  [the longest x3 1.04 us: per_device(): solved = jax.scipy.linalg.solve_triangular(factor, local_factor, lower=True)]
where the time goes in v2:
time: 57.3 us; the launch traced here: 57.1 us
  Pallas kernels  53.6 us (94%)
  local copies, waits for them, and re-layouts  2.77 us (5%)
  between operations  0.66 us (1%)
    pallas_call x1, Pallas kernels, tail(): pl.pallas_call(functools.partial(tail_kernel, groups, tiles), out_shape=(...  22.1 us
    pallas_call x1, Pallas kernels, stencil(): pl.pallas_call(functools.partial(stencil_kernel, groups, tiles), out_shap...  20.9 us
    pallas_call x1, Pallas kernels, solve(): pl.pallas_call(functools.partial(solve_kernel, scale), out_shape=(jax.Sha...  8.71 us
    unnamed x6, local copies, waits for them, and re-layouts  2.77 us
    pallas_call x1, Pallas kernels, pack(): pl.pallas_call(pack_kernel, out_shape=(jax.ShapeDtypeStruct((2 * NYD, ROW...  1.97 us

profile of v2, /device:TPU:1, one launch (start us, length us, event | category | flops | bytes accessed | tf_op | source)
XLA Modules:
  0.0 57.1 jit_solution(12854438393956175177)
XLA Ops:
  0.6 0.0 copy-start
  0.6 1.4 %copy-done = f32[2,192,8,128]{3,2,1,0:T(8,128)S(1)} copy-done((f32[2,192,8,128]{3,2,1,0:T(8,128)S(1)}, f32[2,192,8,128]{3,2,1,0:T(8,128)}, u32[]{:S(2)}) %copy-start) | copy-done | bytes 1572888
  2.0 0.0 copy-start.1
  2.0 0.7 %copy-done.1 = f32[8,128]{1,0:T(8,128)S(1)} copy-done((f32[8,128]{1,0:T(8,128)S(1)}, f32[8,128]{1,0:T(8,128)}, u32[]{:S(2)}) %copy-start.1) | copy-done | bytes 4120
  2.7 0.0 copy-start.2
  2.7 0.7 %copy-done.2 = f32[8,128]{1,0:T(8,128)S(1)} copy-done((f32[8,128]{1,0:T(8,128)S(1)}, f32[8,128]{1,0:T(8,128)}, u32[]{:S(2)}) %copy-start.2) | copy-done | bytes 4120
  3.4 2.0 %pack.1 = (f32[16,200,128]{2,1,0:T(8,128)S(1)}, f32[16,8,128]{2,1,0:T(8,128)S(1)}, f32[16,8,128]{2,1,0:T(8,128)S(1)}) custom-call(f32[3072,128]{1,0:T(8,128)S(1)} %bitcast.2, f32[8,128]{1,0:T(8,128)S(1)} %copy-done.1, f32[8,128]{1,0:T(8,128)S(1)} %copy-done.2), custom_call_target="tpu_custom_call" | custom-call | tf_op jit(solution)/shard_map/pack/pallas_call | solution.py:63
  5.4 20.9 %stencil.1.e_ref = f32[16,192,128]{2,1,0:T(8,128)S(1)} custom-call(f32[16,200,128]{2,1,0:T(8,128)S(1)} %get-tuple-element.9.t_ref, f32[16,8,128]{2,1,0:T(8,128)S(1)} %get-tuple-element.10.left_ref, f32[16,8,128]{2,1,0:T(8,128)S(1)} %get-tuple-element.11.right_ref), custom_call_target="tpu_custom_call" | custom-call | tf_op jit(solution)/shard_map/stencil/pallas_call | solution.py:299
  26.3 22.1 %tail.1 = (f32[192,128]{1,0:T(8,128)S(1)}, f32[192,256]{1,0:T(8,128)S(1)}) custom-call(f32[16,192,128]{2,1,0:T(8,128)S(1)} %stencil.1.e_ref), custom_call_target="tpu_custom_call" | custom-call | tf_op jit(solution)/shard_map/tail/pallas_call | solution.py:536
  48.3 8.7 %solve.1 = (f32[192,192]{1,0:T(8,128)}, f32[1,192]{1,0:T(1,128)}) custom-call(f32[192,128]{1,0:T(8,128)S(1)} %get-tuple-element.12.o_ref, f32[192,256]{1,0:T(8,128)S(1)} %get-tuple-element.13.r_ref), custom_call_target="tpu_custom_call" | custom-call | tf_op jit(solution)/shard_map/solve/pallas_call | solution.py:556
Async XLA Ops:
  0.6 1.4 %copy-start = (f32[2,192,8,128]{3,2,1,0:T(8,128)S(1)}, f32[2,192,8,128]{3,2,1,0:T(8,128)}, u32[]{:S(2)}) copy-start(f32[2,192,8,128]{3,2,1,0:T(8,128)} %param.3) | copy-start | bytes 4718596
  2.0 0.7 %copy-start.1 = (f32[8,128]{1,0:T(8,128)S(1)}, f32[8,128]{1,0:T(8,128)}, u32[]{:S(2)}) copy-start(f32[8,128]{1,0:T(8,128)} %self_ref.1) | copy-start | bytes 12292
  2.7 0.7 %copy-start.2 = (f32[8,128]{1,0:T(8,128)S(1)}, f32[8,128]{1,0:T(8,128)}, u32[]{:S(2)}) copy-start(f32[8,128]{1,0:T(8,128)} %cross_ref.1) | copy-start | bytes 12292

commit v3 on v2

--- a/solution.py
+++ b/solution.py
@@ -14,11 +14,16 @@
 K = 192
 NYD = 8
 LANES = 128
-ROWS = K + 8
-BLOCKS_K = ROWS // 8
-CHUNKS = 5
-CHUNK = ROWS // CHUNKS
-PER_CHUNK = CHUNK // 8
+BLOCKS_K = K // 8
+GROUPS_K = BLOCKS_K // 8
+PER_CHUNK = 4
+CHUNKS = BLOCKS_K // PER_CHUNK
+CHUNK = 8 * PER_CHUNK
+WINDOW = 3
+TOGETHER = 2
+COEF = GROUPS_K
+SLOTS = 2 * GROUPS_K + 1
+PAIRS = ((0, 1), (2, 6), (4, 5), (COEF, None))
 EDGE = STEPS
 EXT = NYD + 2 * EDGE
 DIFFUSION = 0.2
@@ -32,53 +37,11 @@
     return lax.broadcasted_iota(jnp.int32, shape, 1)
 
 
-def pack_kernel(tan_ref, self_ref, cross_ref, t_ref, left_ref, right_ref):
-    lane = lanes_of()
-    sub = lax.broadcasted_iota(jnp.int32, (8, LANES), 0)
-
-    def body(fy, _):
-        f = fy // NYD
-        y = fy - f * NYD
-        base = f * (K * NYD) + y
-        own_self = jnp.broadcast_to(self_ref[pl.ds(y, 1), :], (8, LANES))
-        own_cross = jnp.broadcast_to(cross_ref[pl.ds(y, 1), :], (8, LANES))
-        block = jnp.where(sub == 0, own_self, own_cross)
-        left = jnp.zeros((8, LANES), F32)
-        right = jnp.zeros((8, LANES), F32)
-        for b in range(BLOCKS_K):
-            if b > 0:
-                block = tan_ref[pl.ds(base + 64 * (b - 1), 8, stride=NYD), :]
-            t_ref[fy, 8 * b : 8 * b + 8, :] = block
-            here = (lane >= EDGE * b) & (lane < EDGE * b + EDGE)
-            left = jnp.where(here, pltpu.roll(block, EDGE * b, 1) if b else block, left)
-            right = jnp.where(here, pltpu.roll(block, (EDGE * b + EDGE) % LANES, 1), right)
-        left_ref[fy] = left
-        right_ref[fy] = right
-        return 0
-
-    lax.fori_loop(0, 2 * NYD, body, 0)
-
-
-def pack(tangents, reaction_self, reaction_cross):
-    return pl.pallas_call(
-        pack_kernel,
-        out_shape=(
-            jax.ShapeDtypeStruct((2 * NYD, ROWS, LANES), F32),
-            jax.ShapeDtypeStruct((2 * NYD, 8, LANES), F32),
-            jax.ShapeDtypeStruct((2 * NYD, 8, LANES), F32),
-        ),
-        in_specs=[VMEM_SPEC] * 3,
-        out_specs=[VMEM_SPEC] * 3,
-        compiler_params=pltpu.CompilerParams(vmem_limit_bytes=LIMIT),
-        name="pack",
-    )(tangents.reshape(2 * K * NYD, LANES), reaction_self, reaction_cross)
-
-
-def stencil_kernel(
+def front_kernel(
     groups, tiles,
-    t_ref, left_ref, right_ref, e_ref,
-    up_ref, down_ref, xl_ref, xr_ref, co_ref,
-    row_send, row_recv, edge_send, edge_recv,
+    tan_hbm, self_hbm, cross_hbm, e_ref,
+    cells_ref, cf_ref, o_ref, t_ref, x_ref, q_ref, out_ref, co_ref,
+    local_sem, cf_sem, cf_send, cf_recv, row_send, row_recv, edge_send, edge_recv,
 ):
     g = lax.axis_index("grp")
     t = lax.axis_index("tile")
@@ -94,227 +57,375 @@
         @pl.when(exists(dg, dt))
         def _():
             pl.semaphore_signal(barrier, inc=1, device_id=(g + dg, t + dt), device_id_type=MESH)
+
+    def fields_of(c):
+        return pl.ds(c * CHUNK if isinstance(c, int) else pl.multiple_of(c * CHUNK, 8), CHUNK)
+
+    def local_copy(group):
+        fields = pl.ds(64 * group, 64)
+        return pltpu.make_async_copy(tan_hbm.at[:, fields], cells_ref.at[0, :, fields], local_sem.at[group])
+
+    cf_copies = [
+        pltpu.make_async_copy(src, cf_ref.at[0, i], cf_sem.at[i]) for i, src in enumerate((self_hbm, cross_hbm))
+    ]
+    for copy in cf_copies:
+        copy.start()
+    for group in range(GROUPS_K):
+        local_copy(group).start()
+
+    def row_copies(direction, c):
+        fields = fields_of(c)
+        spans = (slice(0, 4), slice(0, 3)) if direction == 0 else (slice(4, 8), slice(5, 8))
+        return [
+            pltpu.make_async_remote_copy(
+                src_ref=cells_ref.at[0, f, fields, spans[f], :],
+                dst_ref=cells_ref.at[1, f, fields, spans[f], :],
+                send_sem=row_send.at[direction, c, f],
+                recv_sem=row_recv.at[direction, c, f],
+                device_id=(g, t + (1 if direction else -1)),
+                device_id_type=MESH,
+            )
+            for f in range(2)
+        ]
+
+    def cf_copy(direction):
+        return pltpu.make_async_remote_copy(
+            src_ref=cf_ref.at[0],
+            dst_ref=cf_ref.at[1 + direction],
+            send_sem=cf_send.at[direction],
+            recv_sem=cf_recv.at[direction],
+            device_id=(g, t + (1 if direction else -1)),
+            device_id_type=MESH,
+        )
+
+    def edge_copy(side, dt):
+        rows = {-1: slice(0, 4), 0: slice(0, 8), 1: slice(4, 8)}[dt]
+        return pltpu.make_async_remote_copy(
+            src_ref=t_ref.at[rows],
+            dst_ref=x_ref.at[side, 1 - dt, rows],
+            send_sem=edge_send.at[side, 1 - dt],
+            recv_sem=edge_recv.at[side, 1 - dt],
+            device_id=(g + (1 if side else -1), t + dt),
+            device_id_type=MESH,
+        )
+
+    lane = lanes_of()
+    sub = lax.broadcasted_iota(jnp.int32, (8, LANES), 0)
+    within = lane & 15
+    shared = ((lane + EDGE) & 15) < 2 * EDGE
+    cell_rows = cells_ref.reshape(2 * 2 * K * NYD, LANES)
+    halo = 2 * K * NYD
+    top, bottom = t == 0, t == tiles - 1
+
+    def row_of(e):
+        above = e < EDGE
+        below = e >= EDGE + NYD
+        where = jnp.where(above & ~top, 0, jnp.where(below & ~bottom, 2, 1))
+        y = jnp.where(
+            above,
+            jnp.where(top, EDGE - 1 - e, e + NYD - EDGE),
+            jnp.where(below & bottom, EDGE + 2 * NYD - 1 - e, e - EDGE - jnp.where(below, NYD, 0)),
+        )
+        return where, y
+
+    row_at = [
+        (1, e - EDGE) if EDGE <= e < EDGE + NYD else row_of(jnp.int32(e)) for e in range(EXT)
+    ]
+
+    def main_of(f, e, b):
+        base = f * (K * NYD) + 64 * b
+        where, y = row_at[e]
+        if e < EDGE or e >= EDGE + NYD:
+            base = base + jnp.where(where == 1, 0, halo)
+        return cell_rows[pl.ds(base + y, 8, stride=NYD), :]
+
+    def pack_coefs(e):
+        where, y = row_at[e]
+        source = 0 if isinstance(where, int) else jnp.where(where == 1, 0, 2 if e < EDGE else 1)
+        rows = [jnp.broadcast_to(cf_ref[source, i, pl.ds(y, 1), :], (8, LANES)) for i in range(2)]
+        block = jnp.where(sub == 0, rows[0], rows[1])
+        block = jnp.where((lane < 8) | (lane >= LANES - 8), block, 0.0)
+        for shift in (16, 32, 64):
+            block = block + pltpu.roll(block, shift, 1)
+        o_ref[e, COEF] = block
+        own = rows[0]
+        co_ref[0, 0, e] = (own + (1.0 - 4.0 * DIFFUSION)) * (1.0 / DIFFUSION)
+        for s in range(1, STEPS + 1):
+            co_ref[0, s, e] = rows[1] * ((1.0 - SLOW_RATE) ** (s - 1) / DIFFUSION**s)
+
+    for copy in cf_copies:
+        copy.wait()
+    for y in range(NYD):
+        pack_coefs(EDGE + y)
+    for group in range(GROUPS_K):
+        local_copy(group).wait()
+
+        def pack_row(y, _):
+            for f in range(2):
+                packed = None
+                for m in range(8):
+                    block = cell_rows[pl.ds(f * (K * NYD) + 64 * (8 * group + m) + y, 8, stride=NYD), :]
+                    if m == 0:
+                        packed = block
+                    else:
+                        packed = jnp.where(
+                            (lane >= 16 * m - 8) & (lane < 16 * m + 8), pltpu.roll(block, 16 * m, 1), packed
+                        )
+                o_ref[EDGE + y, f * (GROUPS_K + 1) + group] = packed
+            return 0
+
+        lax.fori_loop(0, NYD, pack_row, 0)
+
+    def share_row(y, _):
+        for i, (one, two) in enumerate(PAIRS):
+            value = o_ref[EDGE + y, one]
+            if two is not None:
+                value = jnp.where(shared, value, pltpu.roll(o_ref[EDGE + y, two], 8, 1))
+            t_ref[y, i] = value
+        return 0
+
+    lax.fori_loop(0, NYD, share_row, 0)
+
     wide_g = 1 + (g > 0).astype(jnp.int32) + (g < groups - 1).astype(jnp.int32)
     wide_t = 1 + (t > 0).astype(jnp.int32) + (t < tiles - 1).astype(jnp.int32)
     pl.semaphore_wait(barrier, wide_g * wide_t - 1)
 
-    def row_copies(direction, c):
-        rows = pl.ds(pl.multiple_of(c * CHUNK, 8), CHUNK)
-        if direction == 0:
-            fast, slow, dst, dt = slice(0, 4), slice(8, 11), down_ref, -1
-        else:
-            fast, slow, dst, dt = slice(4, 8), slice(13, 16), up_ref, 1
-        out = []
-        for i, (src, where) in enumerate(((fast, slice(0, 4)), (slow, slice(4, 7)))):
-            out.append(
-                pltpu.make_async_remote_copy(
-                    src_ref=t_ref.at[src, rows, :],
-                    dst_ref=dst.at[where, rows, :],
-                    send_sem=row_send.at[direction, c, i],
-                    recv_sem=row_recv.at[direction, c, i],
-                    device_id=(g, t + dt),
-                    device_id_type=MESH,
-                )
-            )
-        return out
-
-    def edge_copies(side, dt):
-        src = left_ref if side == 0 else right_ref
-        dst = xr_ref if side == 0 else xl_ref
-        dg = -1 if side == 0 else 1
-        rows, where = {
-            -1: (slice(0, 4), slice(12, 16)),
-            0: (slice(0, 8), slice(4, 12)),
-            1: (slice(4, 8), slice(0, 4)),
-        }[dt]
-        out = []
-        for f in range(2):
-            out.append(
-                pltpu.make_async_remote_copy(
-                    src_ref=src.at[slice(8 * f + rows.start, 8 * f + rows.stop)],
-                    dst_ref=dst.at[slice(EXT * f + where.start, EXT * f + where.stop)],
-                    send_sem=edge_send.at[side, dt + 1, f],
-                    recv_sem=edge_recv.at[side, dt + 1, f],
-                    device_id=(g + dg, t + dt),
-                    device_id_type=MESH,
-                )
-            )
-        return dg, out
-
-    for direction, dt in ((0, -1), (1, 1)):
-        @pl.when(has[dt])
-        def _():
-            for copy in row_copies(direction, 0):
-                copy.start()
-    for side in range(2):
-        for dt in (0, -1, 1):
-            dg, copies = edge_copies(side, dt)
-
-            @pl.when(exists(dg, dt))
+    def send(c):
+        for direction in range(2):
+            @pl.when(has[1 if direction else -1])
             def _():
-                for copy in copies:
-                    copy.start()
-    for direction, dt in ((0, -1), (1, 1)):
-        @pl.when(has[dt])
-        def _():
-            def start(c, _):
                 for copy in row_copies(direction, c):
                     copy.start()
-                return 0
-
-            lax.fori_loop(1, CHUNKS, start, 0)
-
-    def wait_rows(c):
-        for direction, dt in ((0, 1), (1, -1)):
-            @pl.when(has[dt])
+
+    def receive(c):
+        for direction in range(2):
+            @pl.when(has[-1 if direction else 1])
             def _():
                 for copy in row_copies(direction, c):
                     copy.wait_recv()
 
-    for side in range(2):
-        for dt in (0, -1, 1):
-            dg, copies = edge_copies(side, dt)
-
-            @pl.when(exists(-dg, -dt))
+    def settle(c):
+        for direction in range(2):
+            @pl.when(has[1 if direction else -1])
             def _():
-                for copy in copies:
-                    copy.wait_recv()
-
-    wait_rows(0)
-
-    lane = lanes_of()
-    zero = jnp.zeros((8, LANES), jnp.int32)
-    first_lane = lane == 0
-    last_lane = lane == LANES - 1
-    wall_left = first_lane & (zero + g == 0)
-    wall_right = last_lane & (zero + g == groups - 1)
-    wall_top = zero + t == 0
-    wall_bottom = zero + t == tiles - 1
-    near = lane < EDGE
-    far = lane >= LANES - EDGE
-
-    def main_of(f, e, b):
-        rows = pl.ds(pl.multiple_of(8 * b, 8), 8)
-        if e < EDGE:
-            return up_ref[e if f == 0 else 4 + e - 1, rows, :]
-        if e < EDGE + NYD:
-            return t_ref[NYD * f + e - EDGE, rows, :]
-        return down_ref[e - 12 + 4 * f, rows, :]
-
-    def halo_of(f, e, b):
-        to_low = lax.rem(LANES - EDGE * b, LANES)
-        to_high = LANES - EDGE - EDGE * b
-        from_right = pltpu.roll(xr_ref[EXT * f + e], to_low, 1)
-        from_left = pltpu.roll(xl_ref[EXT * f + e], to_high, 1)
-        return jnp.where(near, from_right, jnp.where(far, from_left, 0.0))
-
-    for e in range(1, EXT - 1):
-        for part, block in enumerate((main_of(0, e, 0), halo_of(0, e, jnp.int32(0)))):
-            own = jnp.broadcast_to(block[0:1, :], (8, LANES)) + (1.0 - 4.0 * DIFFUSION)
-            co_ref[part, 0, e] = own
-            co_ref[part, 1, e] = jnp.broadcast_to(block[1:2, :], (8, LANES))
-
-    def sides(value):
-        main, halo = value
-        lm, lh = pltpu.roll(main, 1, 1), pltpu.roll(halo, 1, 1)
-        rm, rh = pltpu.roll(main, LANES - 1, 1), pltpu.roll(halo, LANES - 1, 1)
-        left = jnp.where(wall_left, main, jnp.where(first_lane, lh, lm))
-        right = jnp.where(wall_right, main, jnp.where(last_lane, rh, rm))
-        return (
-            left + right,
-            jnp.where(first_lane, lm, lh) + jnp.where(last_lane, rm, rh),
-        )
-
-    def compute(b):
-        fast = [[None] * EXT for _ in range(STEPS + 1)]
-        slow = [[None] * EXT for _ in range(STEPS + 1)]
+                for copy in row_copies(direction, c):
+                    copy.wait_send()
+
+    for direction in range(2):
+        @pl.when(has[1 if direction else -1])
+        def _():
+            cf_copy(direction).start()
+    send(0)
+    for dt in (0, -1, 1):
+        for side in range(2):
+            @pl.when(exists(1 if side else -1, dt))
+            def _():
+                edge_copy(side, dt).start()
+    for c in range(1, WINDOW):
+        send(c)
+    for direction in range(2):
+        @pl.when(has[-1 if direction else 1])
+        def _():
+            cf_copy(direction).wait_recv()
+    for e in range(EXT):
+        if e < EDGE or e >= EDGE + NYD:
+            pack_coefs(e)
+
+    def evolve(loads, coefs, stores):
+        lots = range(len(loads))
+        fast = [[[None] * EXT for _ in range(STEPS + 1)] for _ in lots]
+        slow = [[[None] * EXT for _ in range(STEPS + 1)] for _ in lots]
         for e in range(EXT):
-            fast[0][e] = (main_of(0, e, b), halo_of(0, e, b))
-            if 1 <= e < EXT - 1:
-                slow[0][e] = (main_of(1, e, b), halo_of(1, e, b))
+            for n in lots:
+                fast[n][0][e] = loads[n](0, e)
+                if 1 <= e < EXT - 1:
+                    slow[n][0][e] = loads[n](1, e)
             for s in range(1, STEPS + 1):
                 r = e - s
                 if r < s or r > EXT - 1 - s:
                     continue
-                old, old_slow = fast[s - 1][r], slow[s - 1][r]
-                north, south = fast[s - 1][r - 1], fast[s - 1][r + 1]
-                side = sides(old)
-                new, new_slow = [], []
-                for part in range(2 if s < STEPS else 1):
-                    up, down = north[part], south[part]
-                    if r == EDGE:
-                        up = jnp.where(wall_top, old[part], up)
-                    if r == EDGE + NYD - 1:
-                        down = jnp.where(wall_bottom, old[part], down)
-                    total = (up + down) + side[part]
-                    new.append(
-                        co_ref[part, 0, r] * old[part]
-                        + DIFFUSION * total
-                        + co_ref[part, 1, r] * old_slow[part]
+                drift = SLOW_RATE * DIFFUSION ** (s - 1) / (1.0 - SLOW_RATE) ** s
+                for n in lots:
+                    before = fast[n][s - 1]
+                    old, old_slow = before[r], slow[n][s - 1][r]
+                    total = (before[r - 1] + before[r + 1]) + (
+                        pltpu.roll(old, 1, 1) + pltpu.roll(old, LANES - 1, 1)
                     )
-                    new_slow.append(old_slow[part] + SLOW_RATE * (old[part] - old_slow[part]))
-                fast[s][r] = tuple(new)
-                slow[s][r] = tuple(new_slow)
-                if s == STEPS:
-                    rows = pl.ds(pl.multiple_of(8 * (b - 1), 8), 8)
-                    e_ref[r - EDGE, rows, :] = new[0]
-                    e_ref[NYD + r - EDGE, rows, :] = new_slow[0]
-
-    def chunk(first, count):
-        def body(i, _):
-            compute(first + i)
+                    new = total + (coefs[n](0, r) * old + coefs[n](s, r) * old_slow)
+                    new_slow = old_slow + drift * old
+                    fast[n][s][r] = new
+                    slow[n][s][r] = new_slow
+                    if s == STEPS:
+                        stores[n](r - EDGE, new * DIFFUSION**STEPS)
+                        stores[n](NYD + r - EDGE, new_slow * (1.0 - SLOW_RATE) ** STEPS)
+
+    def block_steps(first):
+        loads, stores = [], []
+        for n in range(TOGETHER):
+            b = first + n
+            group = b // 8
+            m = b - 8 * group
+            rows = pl.ds(pl.multiple_of(8 * b, 8), 8)
+            here = ((lane + 8) & (LANES - 1)) // 16 == m
+
+            def load(f, e, b=b, group=group, m=m, here=here):
+                value = main_of(f, e, b)
+                if e < EDGE or e >= EDGE + NYD:
+                    slot = f * (GROUPS_K + 1) + group
+                    o_ref[e, slot] = jnp.where(here, pltpu.roll(value, 16 * m, 1), o_ref[e, slot])
+                return value
+
+            def store(fy, value, rows=rows):
+                e_ref[fy, rows, :] = value
+
+            loads.append(load)
+            stores.append(store)
+        evolve(loads, [lambda s, r: co_ref[0, s, r]] * TOGETHER, stores)
+
+    def chunk(c, _):
+        receive(c)
+
+        @pl.when(c < CHUNKS - WINDOW)
+        def _():
+            send(c + WINDOW)
+
+        def step(i, _):
+            block_steps(PER_CHUNK * c + TOGETHER * i)
             return 0
 
-        lax.fori_loop(0, count, body, 0)
-
-    chunk(1, PER_CHUNK - 1)
-
-    def rest(c, _):
-        wait_rows(c)
-        chunk(c * PER_CHUNK, PER_CHUNK)
+        lax.fori_loop(0, PER_CHUNK // TOGETHER, step, 0)
         return 0
 
-    lax.fori_loop(1, CHUNKS, rest, 0)
-
-    for direction, dt in ((0, -1), (1, 1)):
-        @pl.when(has[dt])
+    lax.fori_loop(0, CHUNKS, chunk, 0)
+
+    for dt in (0, -1, 1):
+        for side in range(2):
+            @pl.when(exists(-1 if side else 1, -dt))
+            def _():
+                edge_copy(side, dt).wait_recv()
+
+    def join(side, e, slot, value):
+        beside = within < EDGE if side == 0 else within >= 16 - EDGE
+        q_ref[side, e, slot] = jnp.where(beside, value, o_ref[e, slot])
+
+    for side in range(2):
+        @pl.when(hasg[-1 if side else 1])
         def _():
-            def finish(c, _):
-                for copy in row_copies(direction, c):
-                    copy.wait_send()
+            def join_row(k, _):
+                for e in (4 * k, 4 * k + 1, 4 * k + 2, 4 * k + 3):
+                    where, y = row_of(e)
+                    for i, (one, two) in enumerate(PAIRS):
+                        value = x_ref[side, where, y, i]
+                        join(side, e, one, value)
+                        if two is not None:
+                            join(side, e, two, pltpu.roll(value, LANES - 8, 1))
                 return 0
 
-            lax.fori_loop(0, CHUNKS, finish, 0)
-    for side in range(2):
-        for dt in (0, -1, 1):
-            dg, copies = edge_copies(side, dt)
-
-            @pl.when(exists(dg, dt))
+            lax.fori_loop(0, EXT // 4, join_row, 0)
+
+        @pl.when(g == (0 if side else groups - 1))
+        def _():
+            def mirror_row(k, _):
+                for e in (4 * k, 4 * k + 1, 4 * k + 2, 4 * k + 3):
+                    for slot in range(SLOTS):
+                        value = o_ref[e, slot]
+                        flipped = None
+                        for i in range(EDGE):
+                            shift = LANES - 7 + 2 * i if side else 1 + 2 * i
+                            moved = pltpu.roll(value, shift, 1)
+                            flipped = moved if flipped is None else jnp.where((lane & 3) == i, moved, flipped)
+                        join(side, e, slot, flipped)
+                return 0
+
+            lax.fori_loop(0, EXT // 4, mirror_row, 0)
+
+    def side_coefs(k, _):
+        for side, e in [(side, 2 * k - 1 + i) for side in range(2) for i in range(2)]:
+            packed = q_ref[side, e, COEF]
+            own = jnp.broadcast_to(packed[0:1, :], (8, LANES))
+            cross = jnp.broadcast_to(packed[1:2, :], (8, LANES))
+            co_ref[1 + side, 0, e] = (own + (1.0 - 4.0 * DIFFUSION)) * (1.0 / DIFFUSION)
+            for s in range(1, STEPS + 1):
+                co_ref[1 + side, s, e] = cross * ((1.0 - SLOW_RATE) ** (s - 1) / DIFFUSION**s)
+        return 0
+
+    lax.fori_loop(1, EXT // 2, side_coefs, 0)
+
+    def side_step(group, _):
+        loads, coefs, stores = [], [], []
+        for side in range(2):
+            loads.append(lambda f, e, side=side: q_ref[side, e, f * (GROUPS_K + 1) + group])
+            coefs.append(lambda s, r, side=side: co_ref[1 + side, s, r])
+
+            def store(fy, value, side=side):
+                out_ref[side, fy, group] = value
+
+            stores.append(store)
+        evolve(loads, coefs, stores)
+        return 0
+
+    lax.fori_loop(0, GROUPS_K, side_step, 0)
+
+    at_side = (lane < EDGE) | (lane >= LANES - EDGE)
+
+    def merge(i, _):
+        for fy in (4 * i, 4 * i + 1, 4 * i + 2, 4 * i + 3):
+            for group in range(GROUPS_K):
+                value = jnp.where(within < 8, out_ref[1, fy, group], out_ref[0, fy, group])
+                for m in range(8):
+                    rows = slice(64 * group + 8 * m, 64 * group + 8 * m + 8)
+                    moved = pltpu.roll(value, LANES - 16 * m, 1) if m else value
+                    e_ref[fy, rows, :] = jnp.where(at_side, moved, e_ref[fy, rows, :])
+        return 0
+
+    lax.fori_loop(0, NYD // 2, merge, 0)
+
+    def finish(c, _):
+        settle(c)
+        return 0
+
+    lax.fori_loop(0, CHUNKS, finish, 0)
+    for dt in (0, -1, 1):
+        for side in range(2):
+            @pl.when(exists(1 if side else -1, dt))
             def _():
-                for copy in copies:
-                    copy.wait_send()
-
-
-def stencil(groups, tiles, packed, left, right):
+                edge_copy(side, dt).wait_send()
+    for direction in range(2):
+        @pl.when(has[1 if direction else -1])
+        def _():
+            cf_copy(direction).wait_send()
+
+
+def front(groups, tiles, tangents, reaction_self, reaction_cross):
+    hbm = pl.BlockSpec(memory_space=pltpu.HBM)
     return pl.pallas_call(
-        functools.partial(stencil_kernel, groups, tiles),
+        functools.partial(front_kernel, groups, tiles),
         out_shape=jax.ShapeDtypeStruct((2 * NYD, K, LANES), F32),
-        in_specs=[VMEM_SPEC] * 3,
+        in_specs=[hbm] * 3,
         out_specs=VMEM_SPEC,
         scratch_shapes=[
-            pltpu.VMEM((7, ROWS, LANES), F32),
-            pltpu.VMEM((7, ROWS, LANES), F32),
-            pltpu.VMEM((2 * EXT, 8, LANES), F32),
-            pltpu.VMEM((2 * EXT, 8, LANES), F32),
-            pltpu.VMEM((2, 2, EXT, 8, LANES), F32),
+            pltpu.VMEM((2, 2, K, NYD, LANES), F32),
+            pltpu.VMEM((3, 2, NYD, LANES), F32),
+            pltpu.VMEM((EXT, SLOTS, 8, LANES), F32),
+            pltpu.VMEM((NYD, len(PAIRS), 8, LANES), F32),
+            pltpu.VMEM((2, 3, NYD, len(PAIRS), 8, LANES), F32),
+            pltpu.VMEM((2, EXT, SLOTS, 8, LANES), F32),
+            pltpu.VMEM((2, 2 * NYD, GROUPS_K, 8, LANES), F32),
+            pltpu.VMEM((3, STEPS + 1, EXT, 8, LANES), F32),
+            pltpu.SemaphoreType.DMA((GROUPS_K,)),
+            pltpu.SemaphoreType.DMA((2,)),
+            pltpu.SemaphoreType.DMA((2,)),
+            pltpu.SemaphoreType.DMA((2,)),
             pltpu.SemaphoreType.DMA((2, CHUNKS, 2)),
             pltpu.SemaphoreType.DMA((2, CHUNKS, 2)),
-            pltpu.SemaphoreType.DMA((2, 3, 2)),
-            pltpu.SemaphoreType.DMA((2, 3, 2)),
+            pltpu.SemaphoreType.DMA((2, 3)),
+            pltpu.SemaphoreType.DMA((2, 3)),
         ],
-        compiler_params=pltpu.CompilerParams(collective_id=0, has_side_effects=True, vmem_limit_bytes=LIMIT),
-        name="stencil",
-    )(packed, left, right)
+        compiler_params=pltpu.CompilerParams(
+            collective_id=0, has_side_effects=True, vmem_limit_bytes=LIMIT
+        ),
+        name="front",
+    )(*[pltpu.with_memory_space_constraint(x, pltpu.HBM) for x in (tangents, reaction_self, reaction_cross)])
 
 
 def eliminate(w_ref, emit, invert):
@@ -565,8 +676,7 @@
 
 
 def per_device(groups, tiles, tangents, reaction_self, reaction_cross):
-    packed, left, right = pack(tangents, reaction_self, reaction_cross)
-    evolved = stencil(groups, tiles, packed, left, right)
+    evolved = front(groups, tiles, tangents, reaction_self, reaction_cross)
     reduced, local_factor = tail(groups, tiles, evolved)
     corrections, growth = solve(math.sqrt(groups * tiles), reduced, local_factor)
     return (corrections, growth.reshape(K))

time: 57.3 us -> 52.9 us (0.923)
  local copies, waits for them, and re-layouts: 2.77 us -> 0 us
  Pallas kernels: 53.6 us -> 52.2 us
    unnamed x6 -> x0, local copies, waits for them, and re-layouts: 2.77 us -> none
    pallas_call x2 -> x1, Pallas kernels: 22.8 us -> 20.4 us  [front(): pl.pallas_call(functools.partial(front_kernel, groups, tiles), out_shape=...]
    pallas_call x1, Pallas kernels: 22.1 us -> 23 us  [tail(): pl.pallas_call(functools.partial(tail_kernel, groups, tiles), out_shape=(...]
where the time goes in v3:
time: 52.9 us; the launch traced here: 52.8 us
  Pallas kernels  52.2 us (99%)
  between operations  0.65 us (1%)
    pallas_call x1, Pallas kernels, tail(): pl.pallas_call(functools.partial(tail_kernel, groups, tiles), out_shape=(...  23 us
    pallas_call x1, Pallas kernels, front(): pl.pallas_call(functools.partial(front_kernel, groups, tiles), out_shape=...  20.4 us
    pallas_call x1, Pallas kernels, solve(): pl.pallas_call(functools.partial(solve_kernel, scale), out_shape=(jax.Sha...  8.71 us

profile of v3, /device:TPU:1, one launch (start us, length us, event | category | flops | bytes accessed | tf_op | source)
XLA Modules:
  0.0 52.8 jit_solution(15337887385900370851)
XLA Ops:
  0.6 20.4 %front.1.e_ref = f32[16,192,128]{2,1,0:T(8,128)S(1)} custom-call(f32[2,192,8,128]{3,2,1,0:T(8,128)} %tan_hbm.1, f32[8,128]{1,0:T(8,128)} %self_hbm.1, f32[8,128]{1,0:T(8,128)} %cross_hbm.1), custom_call_target="tpu_custom_call" | custom-call | tf_op jit(solution)/shard_map/front/pallas_call | solution.py:401
  21.1 23.0 %tail.1 = (f32[192,128]{1,0:T(8,128)S(1)}, f32[192,256]{1,0:T(8,128)S(1)}) custom-call(f32[16,192,128]{2,1,0:T(8,128)S(1)} %front.1.e_ref), custom_call_target="tpu_custom_call" | custom-call | tf_op jit(solution)/shard_map/tail/pallas_call | solution.py:647
  44.1 8.7 %solve.1 = (f32[192,192]{1,0:T(8,128)}, f32[1,192]{1,0:T(1,128)}) custom-call(f32[192,128]{1,0:T(8,128)S(1)} %get-tuple-element.6.o_ref, f32[192,256]{1,0:T(8,128)S(1)} %get-tuple-element.7.r_ref), custom_call_target="tpu_custom_call" | custom-call | tf_op jit(solution)/shard_map/solve/pallas_call | solution.py:667

commit v4 on v3

--- a/solution.py
+++ b/solution.py
@@ -37,8 +37,8 @@
     return lax.broadcasted_iota(jnp.int32, shape, 1)
 
 
-def front_kernel(
-    groups, tiles,
+def front_part(
+    groups, tiles, greeted,
     tan_hbm, self_hbm, cross_hbm, e_ref,
     cells_ref, cf_ref, o_ref, t_ref, x_ref, q_ref, out_ref, co_ref,
     local_sem, cf_sem, cf_send, cf_recv, row_send, row_recv, edge_send, edge_recv,
@@ -57,6 +57,8 @@
         @pl.when(exists(dg, dt))
         def _():
             pl.semaphore_signal(barrier, inc=1, device_id=(g + dg, t + dt), device_id_type=MESH)
+    for peer in greeted:
+        pl.semaphore_signal(barrier, inc=1, device_id=peer, device_id_type=MESH)
 
     def fields_of(c):
         return pl.ds(c * CHUNK if isinstance(c, int) else pl.multiple_of(c * CHUNK, 8), CHUNK)
@@ -153,13 +155,44 @@
         for s in range(1, STEPS + 1):
             co_ref[0, s, e] = rows[1] * ((1.0 - SLOW_RATE) ** (s - 1) / DIFFUSION**s)
 
+    def send(c):
+        for direction in range(2):
+            @pl.when(has[1 if direction else -1])
+            def _():
+                for copy in row_copies(direction, c):
+                    copy.start()
+
+    def receive(c):
+        for direction in range(2):
+            @pl.when(has[-1 if direction else 1])
+            def _():
+                for copy in row_copies(direction, c):
+                    copy.wait_recv()
+
+    def settle(c):
+        for direction in range(2):
+            @pl.when(has[1 if direction else -1])
+            def _():
+                for copy in row_copies(direction, c):
+                    copy.wait_send()
+
     for copy in cf_copies:
         copy.wait()
+    wide_g = 1 + (g > 0).astype(jnp.int32) + (g < groups - 1).astype(jnp.int32)
+    wide_t = 1 + (t > 0).astype(jnp.int32) + (t < tiles - 1).astype(jnp.int32)
+    pl.semaphore_wait(barrier, wide_g * wide_t - 1 + len(greeted))
+
+    for direction in range(2):
+        @pl.when(has[1 if direction else -1])
+        def _():
+            cf_copy(direction).start()
+    for group in range(GROUPS_K):
+        local_copy(group).wait()
+        for c in range(2 * group, min(2 * group + 2, WINDOW)):
+            send(c)
     for y in range(NYD):
         pack_coefs(EDGE + y)
     for group in range(GROUPS_K):
-        local_copy(group).wait()
-
         def pack_row(y, _):
             for f in range(2):
                 packed = None
@@ -186,43 +219,11 @@
 
     lax.fori_loop(0, NYD, share_row, 0)
 
-    wide_g = 1 + (g > 0).astype(jnp.int32) + (g < groups - 1).astype(jnp.int32)
-    wide_t = 1 + (t > 0).astype(jnp.int32) + (t < tiles - 1).astype(jnp.int32)
-    pl.semaphore_wait(barrier, wide_g * wide_t - 1)
-
-    def send(c):
-        for direction in range(2):
-            @pl.when(has[1 if direction else -1])
-            def _():
-                for copy in row_copies(direction, c):
-                    copy.start()
-
-    def receive(c):
-        for direction in range(2):
-            @pl.when(has[-1 if direction else 1])
-            def _():
-                for copy in row_copies(direction, c):
-                    copy.wait_recv()
-
-    def settle(c):
-        for direction in range(2):
-            @pl.when(has[1 if direction else -1])
-            def _():
-                for copy in row_copies(direction, c):
-                    copy.wait_send()
-
-    for direction in range(2):
-        @pl.when(has[1 if direction else -1])
-        def _():
-            cf_copy(direction).start()
-    send(0)
     for dt in (0, -1, 1):
         for side in range(2):
             @pl.when(exists(1 if side else -1, dt))
             def _():
                 edge_copy(side, dt).start()
-    for c in range(1, WINDOW):
-        send(c)
     for direction in range(2):
         @pl.when(has[-1 if direction else 1])
         def _():
@@ -380,52 +381,23 @@
 
     lax.fori_loop(0, NYD // 2, merge, 0)
 
-    def finish(c, _):
-        settle(c)
-        return 0
-
-    lax.fori_loop(0, CHUNKS, finish, 0)
-    for dt in (0, -1, 1):
-        for side in range(2):
-            @pl.when(exists(1 if side else -1, dt))
+    def drain():
+        def finish(c, _):
+            settle(c)
+            return 0
+
+        lax.fori_loop(0, CHUNKS, finish, 0)
+        for dt in (0, -1, 1):
+            for side in range(2):
+                @pl.when(exists(1 if side else -1, dt))
+                def _():
+                    edge_copy(side, dt).wait_send()
+        for direction in range(2):
+            @pl.when(has[1 if direction else -1])
             def _():
-                edge_copy(side, dt).wait_send()
-    for direction in range(2):
-        @pl.when(has[1 if direction else -1])
-        def _():
-            cf_copy(direction).wait_send()
-
-
-def front(groups, tiles, tangents, reaction_self, reaction_cross):
-    hbm = pl.BlockSpec(memory_space=pltpu.HBM)
-    return pl.pallas_call(
-        functools.partial(front_kernel, groups, tiles),
-        out_shape=jax.ShapeDtypeStruct((2 * NYD, K, LANES), F32),
-        in_specs=[hbm] * 3,
-        out_specs=VMEM_SPEC,
-        scratch_shapes=[
-            pltpu.VMEM((2, 2, K, NYD, LANES), F32),
-            pltpu.VMEM((3, 2, NYD, LANES), F32),
-            pltpu.VMEM((EXT, SLOTS, 8, LANES), F32),
-            pltpu.VMEM((NYD, len(PAIRS), 8, LANES), F32),
-            pltpu.VMEM((2, 3, NYD, len(PAIRS), 8, LANES), F32),
-            pltpu.VMEM((2, EXT, SLOTS, 8, LANES), F32),
-            pltpu.VMEM((2, 2 * NYD, GROUPS_K, 8, LANES), F32),
-            pltpu.VMEM((3, STEPS + 1, EXT, 8, LANES), F32),
-            pltpu.SemaphoreType.DMA((GROUPS_K,)),
-            pltpu.SemaphoreType.DMA((2,)),
-            pltpu.SemaphoreType.DMA((2,)),
-            pltpu.SemaphoreType.DMA((2,)),
-            pltpu.SemaphoreType.DMA((2, CHUNKS, 2)),
-            pltpu.SemaphoreType.DMA((2, CHUNKS, 2)),
-            pltpu.SemaphoreType.DMA((2, 3)),
-            pltpu.SemaphoreType.DMA((2, 3)),
-        ],
-        compiler_params=pltpu.CompilerParams(
-            collective_id=0, has_side_effects=True, vmem_limit_bytes=LIMIT
-        ),
-        name="front",
-    )(*[pltpu.with_memory_space_constraint(x, pltpu.HBM) for x in (tangents, reaction_self, reaction_cross)])
+                cf_copy(direction).wait_send()
+
+    return drain
 
 
 def eliminate(w_ref, emit, invert):
@@ -514,37 +486,12 @@
     return same + mixed + jnp.transpose(mixed)
 
 
-def tail_kernel(
-    groups, tiles,
+def tail_part(
+    groups, tiles, line,
     e_ref, o_ref, r_ref,
     p_ref, near_ref, y_ref, z_ref, w_ref, sends, recvs,
 ):
-    g = lax.axis_index("grp")
-    t = lax.axis_index("tile")
-    inner = 8
-    outer = tiles // inner
-    piece = K // inner
-    z = t // inner
-    q = t - z * inner
-
-    def in_line(d):
-        return (g, z * inner + lax.rem(q + d, inner))
-
-    def in_y(d):
-        return (lax.rem(g + d, groups), t)
-
-    def in_z(d):
-        return (g, lax.rem(z + d, outer) * inner + q)
-
-    peers = (
-        [in_line(d) for d in range(1, inner)]
-        + [in_y(d) for d in range(1, groups)]
-        + [in_z(d) for d in range(1, outer)]
-    )
-    barrier = pltpu.get_barrier_semaphore()
-    for peer in peers:
-        pl.semaphore_signal(barrier, inc=1, device_id=peer, device_id_type=MESH)
-
+    q, g, z, piece, inner, outer, in_line, in_y, in_z = line
     gram = gram_of(e_ref)
     w_ref[:, 0:LANES] = gram[:, 0:LANES]
     w_ref[:, LANES:K] = gram[:, LANES:K]
@@ -552,7 +499,6 @@
     p_ref[0:64, :] = gram[0:64, 0:128]
     p_ref[64:128, :] = jnp.concatenate([gram[0:64, 128:192], gram[64:128, 64:128]], axis=1)
     p_ref[128:192, :] = jnp.concatenate([gram[64:128, 128:192], gram[128:192, 128:192]], axis=1)
-    pl.semaphore_wait(barrier, len(peers))
 
     count = [0]
 
@@ -642,14 +588,62 @@
     )
 
 
-def tail(groups, tiles, evolved):
+def main_kernel(groups, tiles, tan_hbm, self_hbm, cross_hbm, reduced_ref, factor_ref, e_ref, *scratch):
+    g = lax.axis_index("grp")
+    t = lax.axis_index("tile")
+    inner = 8
+    outer = tiles // inner
+    piece = K // inner
+    z = t // inner
+    q = t - z * inner
+
+    def in_line(d):
+        return (g, z * inner + lax.rem(q + d, inner))
+
+    def in_y(d):
+        return (lax.rem(g + d, groups), t)
+
+    def in_z(d):
+        return (g, lax.rem(z + d, outer) * inner + q)
+
+    peers = (
+        [in_line(d) for d in range(1, inner)]
+        + [in_y(d) for d in range(1, groups)]
+        + [in_z(d) for d in range(1, outer)]
+    )
+    line = (q, g, z, piece, inner, outer, in_line, in_y, in_z)
+    front_scratch, tail_scratch = scratch[:16], scratch[16:]
+    drain = front_part(groups, tiles, peers, tan_hbm, self_hbm, cross_hbm, e_ref, *front_scratch)
+    tail_part(groups, tiles, line, e_ref, reduced_ref, factor_ref, *tail_scratch)
+    drain()
+
+
+def run_main(groups, tiles, *arguments):
+    hbm = pl.BlockSpec(memory_space=pltpu.HBM)
     copies = 2 * 7 + (groups - 1) + (tiles // 8 - 1)
     return pl.pallas_call(
-        functools.partial(tail_kernel, groups, tiles),
+        functools.partial(main_kernel, groups, tiles),
         out_shape=(jax.ShapeDtypeStruct((K, LANES), F32), jax.ShapeDtypeStruct((K, 2 * LANES), F32)),
-        in_specs=[VMEM_SPEC],
+        in_specs=[hbm] * 3,
         out_specs=[VMEM_SPEC] * 2,
         scratch_shapes=[
+            pltpu.VMEM((2 * NYD, K, LANES), F32),
+            pltpu.VMEM((2, 2, K, NYD, LANES), F32),
+            pltpu.VMEM((3, 2, NYD, LANES), F32),
+            pltpu.VMEM((EXT, SLOTS, 8, LANES), F32),
+            pltpu.VMEM((NYD, len(PAIRS), 8, LANES), F32),
+            pltpu.VMEM((2, 3, NYD, len(PAIRS), 8, LANES), F32),
+            pltpu.VMEM((2, EXT, SLOTS, 8, LANES), F32),
+            pltpu.VMEM((2, 2 * NYD, GROUPS_K, 8, LANES), F32),
+            pltpu.VMEM((3, STEPS + 1, EXT, 8, LANES), F32),
+            pltpu.SemaphoreType.DMA((GROUPS_K,)),
+            pltpu.SemaphoreType.DMA((2,)),
+            pltpu.SemaphoreType.DMA((2,)),
+            pltpu.SemaphoreType.DMA((2,)),
+            pltpu.SemaphoreType.DMA((2, CHUNKS, 2)),
+            pltpu.SemaphoreType.DMA((2, CHUNKS, 2)),
+            pltpu.SemaphoreType.DMA((2, 3)),
+            pltpu.SemaphoreType.DMA((2, 3)),
             pltpu.VMEM((K, LANES), F32),
             pltpu.VMEM((7, K // 8, LANES), F32),
             pltpu.VMEM((groups, K // 8, LANES), F32),
@@ -658,9 +652,11 @@
             pltpu.SemaphoreType.DMA((copies,)),
             pltpu.SemaphoreType.DMA((copies,)),
         ],
-        compiler_params=pltpu.CompilerParams(collective_id=1, has_side_effects=True, vmem_limit_bytes=LIMIT),
-        name="tail",
-    )(evolved)
+        compiler_params=pltpu.CompilerParams(
+            collective_id=0, has_side_effects=True, vmem_limit_bytes=LIMIT
+        ),
+        name="main",
+    )(*[pltpu.with_memory_space_constraint(x, pltpu.HBM) for x in arguments])
 
 
 def solve(scale, reduced, local_factor):
@@ -676,8 +672,7 @@
 
 
 def per_device(groups, tiles, tangents, reaction_self, reaction_cross):
-    evolved = front(groups, tiles, tangents, reaction_self, reaction_cross)
-    reduced, local_factor = tail(groups, tiles, evolved)
+    reduced, local_factor = run_main(groups, tiles, tangents, reaction_self, reaction_cross)
     corrections, growth = solve(math.sqrt(groups * tiles), reduced, local_factor)
     return (corrections, growth.reshape(K))
 

time: 52.9 us -> 50.2 us (0.949)
  Pallas kernels: 52.2 us -> 49.4 us
    pallas_call x2 -> x1, Pallas kernels: 43.5 us -> 40.7 us  [run_main(): pl.pallas_call(functools.partial(main_kernel, groups, tiles), out_shape=(...]
where the time goes in v4:
time: 50.2 us; the launch traced here: 50 us
  Pallas kernels  49.4 us (98%)
  between operations  0.64 us (1%)
    pallas_call x1, Pallas kernels, run_main(): pl.pallas_call(functools.partial(main_kernel, groups, tiles), out_shape=(...  40.7 us
    pallas_call x1, Pallas kernels, solve(): pl.pallas_call(functools.partial(solve_kernel, scale), out_shape=(jax.Sha...  8.71 us

profile of v4, /device:TPU:1, one launch (start us, length us, event | category | flops | bytes accessed | tf_op | source)
XLA Modules:
  0.0 50.0 jit_solution(5256080576498046721)
XLA Ops:
  0.6 40.7 %main.1 = (f32[192,128]{1,0:T(8,128)S(1)}, f32[192,256]{1,0:T(8,128)S(1)}) custom-call(f32[2,192,8,128]{3,2,1,0:T(8,128)} %tan_hbm.1, f32[8,128]{1,0:T(8,128)} %self_hbm.1, f32[8,128]{1,0:T(8,128)} %cross_hbm.1), custom_call_target="tpu_custom_call" | custom-call | tf_op jit(solution)/shard_map/main/pallas_call | solution.py:624
  41.3 8.7 %solve.1 = (f32[192,192]{1,0:T(8,128)}, f32[1,192]{1,0:T(1,128)}) custom-call(f32[192,128]{1,0:T(8,128)S(1)} %get-tuple-element.6.o_ref, f32[192,256]{1,0:T(8,128)S(1)} %get-tuple-element.7.r_ref), custom_call_target="tpu_custom_call" | custom-call | tf_op jit(solution)/shard_map/solve/pallas_call | solution.py:663

commit v5 on v4

--- a/solution.py
+++ b/solution.py
@@ -19,7 +19,7 @@
 PER_CHUNK = 4
 CHUNKS = BLOCKS_K // PER_CHUNK
 CHUNK = 8 * PER_CHUNK
-WINDOW = 3
+WINDOW = 6
 TOGETHER = 2
 COEF = GROUPS_K
 SLOTS = 2 * GROUPS_K + 1
@@ -28,7 +28,7 @@
 EXT = NYD + 2 * EDGE
 DIFFUSION = 0.2
 SLOW_RATE = 0.05
-LIMIT = 12 << 20
+LIMIT = 20 << 20
 VMEM_SPEC = pl.BlockSpec(memory_space=pltpu.VMEM)
 NEIGHBOURS = [(dg, dt) for dg in (-1, 0, 1) for dt in (-1, 0, 1) if (dg, dt) != (0, 0)]
 

time: 50.2 us -> 49.4 us (0.984)
  Pallas kernels: 49.4 us -> 48.6 us
    pallas_call x1, Pallas kernels: 40.7 us -> 39.9 us  [run_main(): pl.pallas_call(functools.partial(main_kernel, groups, tiles), out_shape=(...]
where the time goes in v5:
time: 49.4 us; the launch traced here: 49.3 us
  Pallas kernels  48.6 us (98%)
  between operations  0.64 us (1%)
    pallas_call x1, Pallas kernels, run_main(): pl.pallas_call(functools.partial(main_kernel, groups, tiles), out_shape=(...  39.9 us
    pallas_call x1, Pallas kernels, solve(): pl.pallas_call(functools.partial(solve_kernel, scale), out_shape=(jax.Sha...  8.71 us

profile of v5, /device:TPU:1, one launch (start us, length us, event | category | flops | bytes accessed | tf_op | source)
XLA Modules:
  0.0 49.3 jit_solution(15810354656526624902)
XLA Ops:
  0.6 39.9 %main.1 = (f32[192,128]{1,0:T(8,128)S(1)}, f32[192,256]{1,0:T(8,128)S(1)}) custom-call(f32[2,192,8,128]{3,2,1,0:T(8,128)} %tan_hbm.1, f32[8,128]{1,0:T(8,128)} %self_hbm.1, f32[8,128]{1,0:T(8,128)} %cross_hbm.1), custom_call_target="tpu_custom_call" | custom-call | tf_op jit(solution)/shard_map/main/pallas_call | solution.py:624
  40.6 8.7 %solve.1 = (f32[192,192]{1,0:T(8,128)}, f32[1,192]{1,0:T(1,128)}) custom-call(f32[192,128]{1,0:T(8,128)S(1)} %get-tuple-element.6.o_ref, f32[192,256]{1,0:T(8,128)S(1)} %get-tuple-element.7.r_ref), custom_call_target="tpu_custom_call" | custom-call | tf_op jit(solution)/shard_map/solve/pallas_call | solution.py:663

commit v6 on v5

--- a/solution.py
+++ b/solution.py
@@ -493,9 +493,6 @@
 ):
     q, g, z, piece, inner, outer, in_line, in_y, in_z = line
     gram = gram_of(e_ref)
-    w_ref[:, 0:LANES] = gram[:, 0:LANES]
-    w_ref[:, LANES:K] = gram[:, LANES:K]
-    w_ref[:, K : 2 * LANES] = jnp.zeros((K, 2 * LANES - K), F32)
     p_ref[0:64, :] = gram[0:64, 0:128]
     p_ref[64:128, :] = jnp.concatenate([gram[0:64, 128:192], gram[64:128, 64:128]], axis=1)
     p_ref[128:192, :] = jnp.concatenate([gram[64:128, 128:192], gram[128:192, 128:192]], axis=1)
@@ -521,7 +518,6 @@
         value = jnp.where(lane + LANES * v >= sub + 8 * p, out, 0.0)
         r_ref[8 * p : 8 * p + 8, LANES * v : LANES * v + LANES] = value
 
-    r_ref[...] = jnp.zeros_like(r_ref)
     local = eliminate(w_ref, emit_factor, False)
 
     def advance(panels):
@@ -532,7 +528,11 @@
     phase = []
     for d in range(1, inner):
         phase.append(copy_to(p_ref.at[rows(lax.rem(q + d, inner))], near_ref.at[d - 1], in_line(d)))
-    advance(6)
+    w_ref[:, 0:LANES] = gram[:, 0:LANES]
+    w_ref[:, LANES:K] = gram[:, LANES:K]
+    w_ref[:, K : 2 * LANES] = jnp.zeros((K, 2 * LANES - K), F32)
+    r_ref[...] = jnp.zeros_like(r_ref)
+    advance(8)
     total = p_ref[rows(q), :]
     for d, copy in enumerate(phase):
         copy.wait_recv()
@@ -541,7 +541,7 @@
     for buf, me, size, peer_of in ((y_ref, g, groups, in_y), (z_ref, z, outer, in_z)):
         buf[me] = total
         phase = [copy_to(buf.at[me], buf.at[me], peer_of(d)) for d in range(1, size)]
-        advance(5)
+        advance(6)
         for copy in phase:
             copy.wait_recv()
         total = buf[0]

time: 49.4 us -> 49.4 us (level)
  no operation moved by 1% of the time
where the time goes in v6:
time: 49.4 us; the launch traced here: 49.3 us
  Pallas kernels  48.6 us (98%)
  between operations  0.64 us (1%)
    pallas_call x1, Pallas kernels, run_main(): pl.pallas_call(functools.partial(main_kernel, groups, tiles), out_shape=(...  39.9 us
    pallas_call x1, Pallas kernels, solve(): pl.pallas_call(functools.partial(solve_kernel, scale), out_shape=(jax.Sha...  8.71 us

profile of v6, /device:TPU:1, one launch (start us, length us, event | category | flops | bytes accessed | tf_op | source)
XLA Modules:
  0.0 49.3 jit_solution(17448090053172928325)
XLA Ops:
  0.6 39.9 %main.1 = (f32[192,128]{1,0:T(8,128)S(1)}, f32[192,256]{1,0:T(8,128)S(1)}) custom-call(f32[2,192,8,128]{3,2,1,0:T(8,128)} %tan_hbm.1, f32[8,128]{1,0:T(8,128)} %self_hbm.1, f32[8,128]{1,0:T(8,128)} %cross_hbm.1), custom_call_target="tpu_custom_call" | custom-call | tf_op jit(solution)/shard_map/main/pallas_call | solution.py:624
  40.6 8.7 %solve.1 = (f32[192,192]{1,0:T(8,128)}, f32[1,192]{1,0:T(1,128)}) custom-call(f32[192,128]{1,0:T(8,128)S(1)} %get-tuple-element.6.o_ref, f32[192,256]{1,0:T(8,128)S(1)} %get-tuple-element.7.r_ref), custom_call_target="tpu_custom_call" | custom-call | tf_op jit(solution)/shard_map/solve/pallas_call | solution.py:663
